TPU v7x, 256 devices: a whole 4x4x8 slice. The times are simulated.
256 devices in a mesh: prow: 16 (over x, y), pcol: 16 (over z, core).
Axes of the slice: x: 4, y: 4, z: 8, core: 2. Of those that a mesh axis runs over, the one named last changes fastest.
Arguments:
- ainv: float32 [16384, 16384], P('prow', 'pcol'), as said below
- panels: float32 [3, 16384, 512], P(None, 'prow', 'pcol'), may hold values from -0.53 to 0.53
- pattern: int32 [3, 128], replicated, may hold values 0 or 1
- coupling: float32 [3, 512, 512], replicated, may hold values from -0.25 to 0.25
- dinv: float32 [3, 512, 512], replicated, as said below
Outputs:
- xpanel: float32 [3, 16384, 512], P(None, 'prow', 'pcol')
- xcross: float32 [3, 512, 512], P(None, 'pcol')
- ydiag: float32 [3, 512, 512], P(None, 'pcol')
Inputs may be any that keep to these rules, and one draw needn't show every extreme that they name: ainv is symmetric: ainv equals its transpose up to rounding. Each dinv[k] is symmetric: it equals its transpose exactly.
All inputs are finite; a program needn't handle non-finite values.
Results may differ from a plain program's by a relative error of at most 0.000092.
Values sent between devices are 32-bit elements; how exact they have to be, the bound alone decides.
A program may use at most 128 MiB of HBM per device.

v0:
```python
import jax
import jax.numpy as jnp
from jax import lax
from jax.sharding import PartitionSpec as P

NB = 128


precise = lax.Precision.HIGHEST


def broadcast(shard, axis, root):
    mine = lax.axis_index(axis) == root
    return lax.psum(jnp.where(mine, shard, jnp.zeros_like(shard)), axis)


def matmul(left, right):
    return jnp.dot(left, right, precision=precise, preferred_element_type=jnp.float32)


def tdot(left, right):
    return lax.dot_general(
        left, right, (((0,), (0,)), ((), ())), precision=precise, preferred_element_type=jnp.float32
    )


def stacked_inner(columns, factor):
    return lax.dot_general(
        columns,
        factor,
        (((1,), (0,)), ((), ())),
        precision=precise,
        preferred_element_type=jnp.float32,
    )


def shards(ainv, panels, pattern, coupling, dinv):
    row_count = lax.axis_size("prow")
    col_count = lax.axis_size("pcol")
    row_index = lax.axis_index("prow")
    col_index = lax.axis_index("pcol")
    local_rows = panels.shape[1]
    local_cols = panels.shape[2]
    cross_rows = ainv.shape[1]
    blocks_here = local_rows // NB
    flags = lax.dynamic_slice_in_dim(pattern, row_index * blocks_here, blocks_here, 1)
    row_mask = jnp.repeat(flags.astype(jnp.float32), NB, axis=1)
    masked = panels * row_mask[:, :, None]
    row_panels = lax.all_gather(masked, "pcol", axis=2, tiled=True)
    ratio = col_count // row_count
    offset = col_index % ratio * cross_rows
    root = col_index // ratio
    first, second, third = (coupling[0], coupling[1], coupling[2])
    my_start = col_index * local_cols

    def own_rows(matrix):
        return lax.dynamic_slice_in_dim(matrix, my_start, local_cols, 0)

    finished = []
    inner = []
    for section in range(3):
        sent = row_panels[section]
        crossed = broadcast(sent, "prow", root)
        partial_value = matmul(ainv, crossed)
        if section == 1:
            partial_value = partial_value + matmul(finished[0], own_rows(first))
        if section == 2:
            partial_value = (
                partial_value
                + matmul(finished[0], own_rows(second))
                + matmul(finished[1], own_rows(third))
            )
        current = -lax.psum_scatter(partial_value, "pcol", scatter_dimension=1, tiled=True)
        finished.append(current)
        terms = stacked_inner(jnp.stack(finished, 0), row_panels[section])
        summed = lax.psum(terms, "prow")
        inner.append(lax.all_gather(summed, "pcol", axis=1, tiled=True))
    result = jnp.stack(finished, 0)
    diag_zero = dinv[0] - inner[0][0].T
    cross_one = -(inner[1][0] + matmul(diag_zero, first))
    diag_one = dinv[1] - inner[1][1].T - tdot(first, cross_one)
    cross_two = -(inner[2][0] + matmul(diag_zero, second) + matmul(cross_one, third))
    cross_three = -(inner[2][1] + tdot(cross_one, second) + matmul(diag_one, third))
    diag_two = dinv[2] - inner[2][2].T - tdot(second, cross_two) - tdot(third, cross_three)
    xcross = lax.dynamic_slice_in_dim(
        jnp.stack([cross_one, cross_two, cross_three], 0), my_start, local_cols, 1
    )
    ydiag = lax.dynamic_slice_in_dim(
        jnp.stack([diag_zero, diag_one, diag_two], 0), my_start, local_cols, 1
    )
    return (result, xcross, ydiag)


def solution(mesh):
    placed = (P("prow", "pcol"), P(None, "prow", "pcol"), P(), P(), P())
    return jax.shard_map(
        shards,
        mesh=mesh,
        in_specs=placed,
        out_specs=(P(None, "prow", "pcol"), P(None, "pcol", None), P(None, "pcol", None)),
        check_vma=False,
    )
```

profile of v0, /device:TPU:1, one launch (start us, length us, event | category | flops | bytes accessed | tf_op | source)
XLA Modules:
  0.0 689.6 jit_solution(7488931692287001959)
XLA Ops:
  7.2 0.0 all-gather.5.cloned.1.call-start
  7.2 0.8 fusion.50
  8.0 0.1 broadcast_bitcast_fusion
  8.1 1.8 broadcast_multiply_fusion
  9.8 0.0 all-gather.5.cloned.1.call-update
  9.9 0.0 all-reduce.7.cloned.1.call-start
  9.9 50.7 %all-gather.5.cloned.1.call-done = f32[3,1024,512]{1,2,0:T(8,128)} async-done(((f32[3,1024,32]{1,2,0:T(8,128)}), f32[3,1024,512]{1,2,0:T(8,128)}) %all-gather.5.cloned.1.call-update) | async-done | bytes 6291472 | tf_op jit(solution)/shard_map/all_gather | solution.py:49
  60.7 5.8 fusion.64
  66.5 3.0 copy.30
  69.5 1.8 copy.31
  71.3 1.9 copy.29
  73.2 1.6 bitcast_select_fusion.2
  74.8 0.7 copy-done.9
  75.5 0.6 copy-done.10
  76.2 2.5 bitcast_select_fusion
  78.7 0.0 reduce-scatter.4.cloned.1.call-start
  78.7 130.7 %all-reduce.7.cloned.1.call-done = (f32[1024,512]{1,0:T(8,128)}, f32[1024,512]{1,0:T(8,128)}, f32[1024,512]{1,0:T(8,128)}) async-done(((f32[1024,512]{1,0:T(8,128)}, f32[1024,512]{1,0:T(8,128)}, f32[1024,512]{1,0:T(8,128)}), (f32[1024,512]{1,0:T(8,128)}, f32[1024,512]{1,0:T(8,128)}, f32[1024,512]{1,0:T(8,128)})) %all-reduce.7.cloned.1.call-update) | async-done | bytes 6291472 | tf_op jit(solution)/shard_map/psum | solution.py:14
  209.4 16.8 %convolution_bitcast_fusion = f32[1024,512]{0,1:T(8,128)} fusion(f32[1024,512]{1,0:T(8,128)} %get-tuple-element.12, f32[1024,1024]{1,0:T(8,128)} %param.5), kind=kOutput, calls=%fused_computation.18 | convolution fusion | flops 6442450944 | bytes 8388608 | tf_op jit(solution)/shard_map/dot_general | solution.py:18
  226.2 0.6 reduce-scatter.6.cloned.1.call-start
  226.8 1.7 fusion.66
  228.5 55.0 %reduce-scatter.4.cloned.1.call-done = f32[1024,32]{0,1:T(8,128)} async-done(((f32[1024,512]{0,1:T(8,128)}), f32[1024,32]{0,1:T(8,128)}) %reduce-scatter.4.cloned.1.call-update) | async-done | bytes 131088 | tf_op jit(solution)/shard_map/reduce_scatter | solution.py:73
  283.5 2.9 fusion.39
  286.4 16.4 %bitcast_add_fusion.1 = f32[1024,512]{0,1:T(8,128)} fusion(f32[1024,512]{0,1:T(8,128)S(1)} %fusion.39, f32[1024,512]{1,0:T(8,128)S(1)} %copy-done.16, f32[1024,1024]{1,0:T(8,128)} %param.5), kind=kOutput, calls=%fused_computation.15 | convolution fusion | flops 6442975232 | bytes 10485760 | tf_op jit(solution)/shard_map/dot_general | solution.py:18
  302.8 0.2 reduce-scatter.8.cloned.1.call-start
  303.1 0.7 copy-done.18
  303.7 4.1 fusion.37
  307.8 53.9 %reduce-scatter.6.cloned.1.call-done = f32[1024,32]{0,1:T(8,128)} async-done(((f32[1024,512]{0,1:T(8,128)}), f32[1024,32]{0,1:T(8,128)}) %reduce-scatter.6.cloned.1.call-update) | async-done | bytes 131088 | tf_op jit(solution)/shard_map/reduce_scatter | solution.py:73
  361.7 2.9 fusion.34
  364.6 16.7 %fusion.6 = f32[1024,512]{0,1:T(8,128)} fusion(f32[1024,512]{0,1:T(8,128)S(1)} %fusion.34, f32[1024,512]{0,1:T(8,128)S(1)} %copy-done.11, f32[1024,512]{1,0:T(8,128)} %get-tuple-element.14, f32[1024,1024]{1,0:T(8,128)} %param.5), kind=kOutput, calls=%fused_computation.13 | convolution fusion | flops 6443499520 | bytes 12582912 | tf_op jit(solution)/shard_map/dot_general | solution.py:18
  381.3 0.0 all-reduce.5.cloned.1.call-start
  381.4 4.2 fusion.14
  385.6 0.6 copy-done.20
  386.2 0.7 copy-done.21
  386.9 4.3 fusion.4
  391.2 48.9 %reduce-scatter.8.cloned.1.call-done = f32[1024,32]{0,1:T(8,128)} async-done(((f32[1024,512]{0,1:T(8,128)}), f32[1024,32]{0,1:T(8,128)}) %reduce-scatter.8.cloned.1.call-update) | async-done | bytes 131088 | tf_op jit(solution)/shard_map/reduce_scatter | solution.py:73
  440.1 0.9 negate_bitcast_fusion
  441.1 1.0 pad_maximum_fusion
  442.1 4.5 fusion
  446.6 0.0 all-gather.9.cloned.1.call-start
  446.7 95.0 %all-reduce.5.cloned.1.call-done = (f32[2,32,512]{2,1,0:T(8,128)}, f32[1,32,512]{2,1,0:T(8,128)}, f32[3,32,512]{2,1,0:T(8,128)}) async-done(((f32[2,32,512]{2,1,0:T(8,128)}, f32[1,32,512]{2,1,0:T(8,128)}, f32[3,32,512]{2,1,0:T(8,128)}), (f32[2,32,512]{2,1,0:T(8,128)}, f32[1,32,512]{2,1,0:T(8,128)}, f32[3,32,512]{2,1,0:T(8,128)})) %all-reduce.5.cloned.1.call-update) | async-done | bytes 393232 | tf_op jit(solution)/shard_map/psum | solution.py:76
  541.7 0.0 all-gather.7.cloned.1.call-start
  541.7 0.7 all-gather.7.cloned.1.call-update
  542.4 0.3 all-gather.11.cloned.1.call-start
  542.7 0.5 all-gather.11.cloned.1.call-update
  543.2 3.6 fusion.65
  546.7 2.6 copy.32
  549.4 2.5 copy.34
  551.9 2.5 copy.33
  554.4 29.6 %all-gather.9.cloned.1.call-done = f32[1,512,512]{2,1,0:T(8,128)} async-done(((f32[1,32,512]{2,1,0:T(8,128)}), f32[1,512,512]{2,1,0:T(8,128)}) %all-gather.9.cloned.1.call-update) | async-done | bytes 1048592 | tf_op jit(solution)/shard_map/all_gather | solution.py:77
  584.0 2.7 fusion.52
  586.8 37.2 %all-gather.7.cloned.1.call-done = f32[2,512,512]{2,1,0:T(8,128)} async-done(((f32[2,32,512]{2,1,0:T(8,128)}), f32[2,512,512]{2,1,0:T(8,128)}) %all-gather.7.cloned.1.call-update) | async-done | bytes 2097168 | tf_op jit(solution)/shard_map/all_gather | solution.py:77
  623.9 4.0 fusion.13
  627.9 1.0 copy-done.1
  628.9 3.0 fusion.11
  631.9 32.9 %all-gather.11.cloned.1.call-done = f32[3,512,512]{2,1,0:T(8,128)} async-done(((f32[3,32,512]{2,1,0:T(8,128)}), f32[3,512,512]{2,1,0:T(8,128)}) %all-gather.11.cloned.1.call-update) | async-done | bytes 3145744 | tf_op jit(solution)/shard_map/all_gather | solution.py:77
  664.8 3.8 convolution_add_fusion.3
  668.7 1.9 fusion.12
  670.5 1.9 convolution_add_fusion.1
  672.5 2.2 fusion.10
  674.7 1.9 fusion.9
  676.7 1.9 fusion.8
  678.6 1.1 fusion.28
  679.8 2.1 copy.25
  681.9 0.7 fusion.33
  (49 shorter events, 0.2 us)
Async XLA Ops:
  7.2 53.5 %all-gather.5.cloned.1.call-start = ((), (), s32[]{:S(2)}) async-start(), calls=%async_computation.3 | async-start | bytes 6684672 | tf_op jit(solution)/shard_map/all_gather | solution.py:49
  9.9 199.6 %all-reduce.7.cloned.1.call-start = ((), (), s32[]{:S(2)}) async-start(), calls=%async_computation.11 | async-start | bytes 12582912 | tf_op jit(solution)/shard_map/psum | solution.py:14
  73.2 2.3 copy-start.9
  73.2 3.0 copy-start.10
  78.7 204.8 %reduce-scatter.4.cloned.1.call-start = ((), (), s32[]{:S(2)}) async-start(), calls=%async_computation.4 | async-start | bytes 2228224 | tf_op jit(solution)/shard_map/reduce_scatter | solution.py:73
  209.4 17.4 %copy-start = (f32[3,512,512]{2,1,0:T(8,128)S(1)}, f32[3,512,512]{2,1,0:T(8,128)}, u32[]{:S(2)}) copy-start(f32[3,512,512]{2,1,0:T(8,128)} %param.8) | copy-start | bytes 9437188
  226.2 135.4 %reduce-scatter.6.cloned.1.call-start = ((), (), s32[]{:S(2)}) async-start(), calls=%async_computation.5 | async-start | bytes 2228224 | tf_op jit(solution)/shard_map/reduce_scatter | solution.py:73
  283.5 2.9 copy-start.16
  302.8 0.9 copy-start.18
  302.8 137.3 %reduce-scatter.8.cloned.1.call-start = ((), (), s32[]{:S(2)}) async-start(), calls=%async_computation.6 | async-start | bytes 2228224 | tf_op jit(solution)/shard_map/reduce_scatter | solution.py:73
  361.7 2.9 copy-start.11
  381.3 4.3 copy-start.22
  381.3 160.4 %all-reduce.5.cloned.1.call-start = ((), (), s32[]{:S(2)}) async-start(), calls=%async_computation.10 | async-start | bytes 786432 | tf_op jit(solution)/shard_map/psum | solution.py:76
  385.6 0.7 copy-start.20
  386.2 0.7 copy-start.21
  442.1 104.7 %copy-start.19 = (f32[3,1024,32]{1,2,0:T(8,128)}, f32[3,1024,32]{1,2,0:T(8,128)S(1)}, u32[]{:S(2)}) copy-start(f32[3,1024,32]{1,2,0:T(8,128)S(1)} %pad_maximum_fusion) | copy-start | bytes 1179652
  446.6 137.4 %all-gather.9.cloned.1.call-start = ((), (), s32[]{:S(2)}) async-start(), calls=%async_computation.8 | async-start | bytes 1114112 | tf_op jit(solution)/shard_map/all_gather | solution.py:77
  541.7 82.2 %all-gather.7.cloned.1.call-start = ((), (), s32[]{:S(2)}) async-start(), calls=%async_computation.7 | async-start | bytes 2228224 | tf_op jit(solution)/shard_map/all_gather | solution.py:77
  542.4 122.3 %all-gather.11.cloned.1.call-start = ((), (), s32[]{:S(2)}) async-start(), calls=%async_computation.9 | async-start | bytes 3342336 | tf_op jit(solution)/shard_map/all_gather | solution.py:77
  623.9 4.9 copy-start.13
  623.9 4.9 copy-start.17
  627.9 1.0 copy-start.1
  664.8 3.9 copy-start.2
  668.6 1.9 copy-start.15
  670.5 4.2 copy-start.4
  670.5 2.0 copy-start.6
  672.5 2.2 copy-start.12
  674.7 1.9 copy-start.7
  676.7 1.9 copy-start.14
  678.6 3.3 copy-start.3
  678.6 3.3 copy-start.5
  678.6 3.3 copy-start.8
Sparse Core Ops, SparseCore 0:
  10.4 50.2 all-gather.4
  78.8 130.5 all-reduce.6
  226.4 57.0 reduce-scatter.3
  303.0 58.6 reduce-scatter.5
  381.4 58.6 reduce-scatter.7
  446.8 94.8 all-reduce.4
  543.5 40.4 all-gather.8
  585.9 38.0 all-gather.6
  625.8 38.9 all-gather.10
where the time goes:
time: 697 us; the launch traced here: 690 us
  waiting for transfers between devices  535 us (77%)
  matrix products  93.4 us (13%)
  local copies, waits for them, and re-layouts  32 us (5%)
  between operations  14.6 us (2%)
  other arithmetic  13.1 us (2%)
    reduce_scatter x3, waiting for transfers between devices, shards(): lax.psum_scatter(partial_value, 'pcol', scatter_dimension=1, tiled=True)  158 us
    psum x1, waiting for transfers between devices, broadcast(): return lax.psum(jnp.where(mine, shard, jnp.zeros_like(shard)), axis)  131 us
    all_gather x3, waiting for transfers between devices, shards(): inner.append(lax.all_gather(summed, 'pcol', axis=1, tiled=True))  99.7 us
    psum x1, waiting for transfers between devices, shards(): summed = lax.psum(terms, 'prow')  95 us
    dot_general x10, matrix products, matmul(): jnp.dot(left, right, precision=precise, preferred_element_type=jnp.float32)  71.6 us
    all_gather x1, waiting for transfers between devices, shards(): row_panels = lax.all_gather(masked, 'pcol', axis=2, tiled=True)  50.7 us
    unnamed x55, local copies, waits for them, and re-layouts  20.9 us
  transfers between devices with their start and end apart: 9, of which 9 were waited for; matrix products, arithmetic and copies ran while one was open for 5% of the time, Pallas kernels for 0%

commit v1 on v0

v1 whole, which is shorter than its diff:
```python
import jax
import jax.numpy as jnp
from jax import lax
from jax.sharding import PartitionSpec as P

NB = 128

high = lax.Precision.HIGH
highest = lax.Precision.HIGHEST


def mm(left, right, precision=high):
    return jnp.dot(left, right, precision=precision, preferred_element_type=jnp.float32)


def tmm(left, right, precision=high):
    return lax.dot_general(
        left, right, (((0,), (0,)), ((), ())), precision=precision, preferred_element_type=jnp.float32
    )


def mmt(left, right, precision=high):
    return lax.dot_general(
        left, right, (((1,), (1,)), ((), ())), precision=precision, preferred_element_type=jnp.float32
    )


def shards(ainv, panels, pattern, coupling, dinv):
    rows = lax.axis_size("prow")
    cols = lax.axis_size("pcol")
    row_index = lax.axis_index("prow")
    col_index = lax.axis_index("pcol")
    count, depth, width = panels.shape
    blocks_here = depth // NB
    flags = lax.dynamic_slice_in_dim(pattern, row_index * blocks_here, blocks_here, 1)
    row_mask = jnp.repeat(flags.astype(jnp.float32), NB, axis=1)
    factors = jnp.swapaxes(panels, 1, 2) * row_mask[:, None, :]
    f0, f1, f2 = lax.all_gather(factors, "pcol", axis=1, tiled=True)
    c0, c1, c2 = coupling[0], coupling[1], coupling[2]
    u01 = -c0
    u12 = -c2
    u02 = mm(c0, c2, highest) - c1
    h0 = f0
    h1 = f1 + tmm(u01, f0)
    h2 = f2 + tmm(u02, f0) + tmm(u12, f1)
    ht = jnp.concatenate([h0, h1, h2], 0)
    partial = mm(ht, ainv).reshape(count, rows, width, depth)
    mine = lax.psum_scatter(partial, "prow", scatter_dimension=1, tiled=False)
    perm = [(r * cols + c, c * cols + r) for r in range(rows) for c in range(cols)]
    xt = -lax.ppermute(mine, ("prow", "pcol"), perm)
    inner0 = mmt(xt[0], ht)
    inner1 = mmt(xt[1], ht[512:])
    inner2 = mmt(xt[2], ht[1024:])
    summed = lax.psum(jnp.concatenate([inner0, inner1, inner2], 1), "prow")
    start = col_index * width

    def own(matrix, axis):
        return lax.dynamic_slice_in_dim(matrix, start, width, axis)

    d0 = own(dinv[0], 0)
    a01 = tmm(own(u01, 1), dinv[0], highest)
    a02 = tmm(own(u02, 1), dinv[0], highest)
    b1 = own(dinv[1], 0)
    b12 = tmm(own(u12, 1), dinv[1], highest)
    y0 = d0 - summed[:, 0:512]
    e01 = mm(d0, u01, highest) - summed[:, 512:1024]
    e02 = mm(d0, u02, highest) - summed[:, 1024:1536]
    y1 = b1 + mm(a01, u01, highest) - summed[:, 1536:2048]
    e12 = mm(a01, u02, highest) + mm(b1, u12, highest) - summed[:, 2048:2560]
    y2 = own(dinv[2], 0) + mm(a02, u02, highest) + mm(b12, u12, highest) - summed[:, 2560:3072]
    return jnp.swapaxes(xt, 1, 2), jnp.stack([e01, e02, e12], 0), jnp.stack([y0, y1, y2], 0)


def solution(mesh):
    placed = (P("prow", "pcol"), P(None, "prow", "pcol"), P(), P(), P())
    return jax.shard_map(
        shards,
        mesh=mesh,
        in_specs=placed,
        out_specs=(P(None, "prow", "pcol"), P(None, "pcol", None), P(None, "pcol", None)),
        check_vma=False,
    )
```

time: 697 us -> 338 us (0.48)
  waiting for transfers between devices: 535 us -> 245 us
  matrix products: 93.4 us -> 53.1 us
  local copies, waits for them, and re-layouts: 32 us -> 12.9 us
    reduce_scatter x3 -> x0, waiting for transfers between devices: 158 us -> none  [shards(): lax.psum_scatter(partial_value, 'pcol', scatter_dimension=1, tiled=True)]
    all_gather x4 -> x1, waiting for transfers between devices: 150 us -> 44.5 us  [shards(): f0, f1, f2 = lax.all_gather(factors, 'pcol', axis=1, tiled=True)]
    psum x2 -> x1, waiting for transfers between devices: 226 us -> 121 us  [shards(): summed = lax.psum(jnp.concatenate([inner0, inner1, inner2], 1), 'prow')]
    unnamed x9 -> x4, waiting for transfers between devices: 1.28 us -> 79.2 us
    dot_general x17 -> x18, matrix products: 93.4 us -> 53.1 us  [the longest x9 32.8 us: mm(): jnp.dot(left, right, precision=precision, preferred_element_type=jnp.floa...]
    unnamed x55 -> x21, local copies, waits for them, and re-layouts: 20.9 us -> 1.92 us
    slice x3, local copies, waits for them, and re-layouts: 11.1 us -> 3.75 us  [the longest x1 3.74 us: shards(): dinv[2]]
  transfers between devices with their start and end apart: 9 -> 4, of which waited for: 9 -> 3; matrix products, arithmetic and copies ran while one was open for 5% -> 6% of each run, Pallas kernels for 0% -> 0%
where the time goes in v1:
time: 338 us; the launch traced here: 337 us
  waiting for transfers between devices  245 us (72%)
  matrix products  53.1 us (16%)
  between operations  14 us (4%)
  local copies, waits for them, and re-layouts  12.9 us (4%)
  other arithmetic  7.1 us (2%)
  starting transfers between devices  5.43 us (2%)
    psum x1, waiting for transfers between devices, shards(): summed = lax.psum(jnp.concatenate([inner0, inner1, inner2], 1), 'prow')  121 us
    unnamed x4, waiting for transfers between devices  79.2 us
    all_gather x1, waiting for transfers between devices, shards(): f0, f1, f2 = lax.all_gather(factors, 'pcol', axis=1, tiled=True)  44.5 us
    dot_general x9, matrix products, mm(): jnp.dot(left, right, precision=precision, preferred_element_type=jnp.floa...  32.8 us
    dot_general x6, matrix products, tmm(): lax.dot_general(left, right, (((0,), (0,)), ((), ())), precision=precisio...  14.2 us
  transfers between devices with their start and end apart: 4, of which 3 were waited for; matrix products, arithmetic and copies ran while one was open for 6% of the time, Pallas kernels for 0%

profile of v1, /device:TPU:1, one launch (start us, length us, event | category | flops | bytes accessed | tf_op | source)
XLA Modules:
  0.0 337.1 jit_solution(12168469248919959419)
XLA Ops:
  7.2 0.0 slice-start
  7.2 0.0 all-gather.2.cloned.1.call-start
  7.2 0.8 dynamic-slice_convert_fusion
  8.1 0.1 broadcast_bitcast_fusion
  8.1 1.8 multiply_bitcast_fusion
  9.9 0.0 all-gather.2.cloned.1.call-update
  10.0 0.0 reduce-scatter.4.cloned.1.call-start
  10.0 0.0 slice-done
  10.0 1.3 copy.12
  11.3 0.0 copy-start
  11.3 4.8 %convolution_subtract_fusion = f32[512,512]{0,1:T(8,128)} fusion(f32[1,512,512]{1,2,0:T(8,128)} %copy.12, f32[3,512,512]{2,1,0:T(8,128)} %param.8), kind=kOutput, calls=%fused_computation.14 | convolution fusion | flops 1610874880 | bytes 4194304 | tf_op jit(solution)/shard_map/dot_general | solution.py:13
  16.1 44.5 %all-gather.2.cloned.1.call-done = f32[3,512,1024]{2,1,0:T(8,128)} async-done(((f32[3,32,1024]{2,1,0:T(8,128)}), f32[3,512,1024]{2,1,0:T(8,128)}) %all-gather.2.cloned.1.call-update) | async-done | bytes 6291472 | tf_op jit(solution)/shard_map/all_gather | solution.py:38
  60.7 0.0 copy-done
  60.7 0.0 copy-start.5
  60.7 4.3 %bitcast_add_fusion = f32[512,1024]{1,0:T(8,128)S(1)} fusion(f32[3,512,1024]{2,1,0:T(8,128)} %all-gather.2.cloned.1.call-done, f32[3,512,512]{2,1,0:T(8,128)S(1)} %copy-done), kind=kOutput, calls=%fused_computation.12 | convolution fusion | flops 1611399168 | bytes 7340032 | tf_op jit(solution)/shard_map/dot_general | solution.py:17
  65.0 0.0 copy-start.6
  65.0 0.0 copy-start.1
  65.0 4.0 %slice_bitcast_fusion.2 = f32[512,1024]{1,0:T(8,128)} fusion(f32[3,512,1024]{2,1,0:T(8,128)} %all-gather.2.cloned.1.call-done), kind=kLoop, calls=%fused_computation.11 | loop fusion | bytes 4194304 | tf_op jit(solution)/shard_map/unstack | solution.py:38
  69.0 0.0 copy-done.5
  69.0 0.0 copy-done.1
  69.0 1.9 fusion.62
  70.9 2.0 fusion.7
  73.0 0.0 copy-done.6
  73.0 0.0 copy-start.3
  73.0 16.0 %fusion.1 = f32[1536,1024]{1,0:T(8,128)S(1)} fusion(f32[1024,1024]{1,0:T(8,128)} %param.5, f32[512,1024]{1,0:T(8,128)S(1)} %fusion.7, f32[512,1024]{1,0:T(8,128)S(1)} %bitcast_add_fusion, f32[512,1024]{1,0:T(8,128)} %slice_bitcast_fusion.2), kind=kOutput, calls=%fused_computation.2 | convolution fusion | flops 9666822144 | bytes 16777216 | tf_op jit(solution)/shard_map/dot_general | solution.py:13
  89.0 0.0 copy-done.3
  89.0 3.2 copy.11
  92.3 0.0 reduce-scatter.4.cloned.1.call-update
  92.3 0.0 all-reduce.3.cloned.1.call-start
  92.4 0.0 copy-start.2
  92.4 1.3 bitcast_negate_fusion
  93.6 2.0 fusion.21
  95.6 0.0 copy-done.2
  95.6 1.0 fusion.65
  96.7 79.2 %reduce-scatter.4.cloned.1.call-done = f32[3,1,32,1024]{3,2,0,1:T(8,128)} async-done(((f32[3,16,32,1024]{3,2,0,1:T(8,128)}), f32[3,1,32,1024]{3,2,0,1:T(8,128)}) %reduce-scatter.4.cloned.1.call-update) | async-done | bytes 393232
  175.8 5.3 %collective-permute-start = (f32[3,32,1024]{2,1,0:T(8,128)}, f32[3,32,1024]{2,1,0:T(8,128)S(1)}, u32[]{:S(2)}, u32[]{:S(2)}) collective-permute-start(f32[3,32,1024]{2,1,0:T(8,128)} %bitcast.108), channel_id=1, source_target_pairs={{0,0},{1,16},{2,32},{3,48},{4,64},{5,80},{6,96},{7,112},{8,128},{9... | collective-permute-start | bytes 1179656 | tf_op jit(solution)/shard_map/ppermute | solution.py:50
  181.2 2.0 fusion.19
  183.1 0.0 copy-start.4
  183.1 0.0 copy-start.7
  183.2 0.0 copy-start.8
  183.2 3.7 %fusion.63 = (f32[1,512,512]{2,1,0:T(8,128)}, f32[1,512,512]{2,1,0:T(8,128)}, f32[1,512,512]{2,1,0:T(8,128)}) fusion(f32[3,512,512]{2,1,0:T(8,128)} %param.9), kind=kLoop, calls=%fused_computation.89 | loop fusion | bytes 6291456 | tf_op jit(solution)/shard_map/slice | solution.py:70
  186.9 0.0 collective-permute-done
  186.9 0.8 fusion.64
  187.7 0.0 copy-done.4
  187.7 0.0 copy-done.7
  187.7 0.5 copy-done.8
  188.2 3.0 fusion
  191.2 2.0 fusion.2
  193.2 1.1 fusion.41
  194.3 0.8 pad_maximum_fusion.3
  195.1 0.0 all-reduce.3.cloned.1.call-update
  195.1 2.1 fusion.17
  197.1 2.3 convolution_add_fusion.1
  199.4 120.8 %all-reduce.3.cloned.1.call-done = f32[32,3072]{1,0:T(8,128)} async-done(((f32[32,3072]{1,0:T(8,128)}), f32[32,3072]{1,0:T(8,128)}) %all-reduce.3.cloned.1.call-update) | async-done | bytes 393232 | tf_op jit(solution)/shard_map/psum | solution.py:54
  320.2 2.3 fusion.15
  322.5 1.6 fusion.16
  324.1 0.9 fusion.42
  325.0 1.6 fusion.12
  326.6 1.6 fusion.14
  328.2 1.6 fusion.10
  329.8 0.8 pad_maximum_fusion.4
  (1 shorter events, 0.0 us)
Async XLA Ops:
  7.2 2.8 slice-start
  7.2 53.5 %all-gather.2.cloned.1.call-start = ((), (), s32[]{:S(2)}) async-start(), calls=%async_computation.1 | async-start | bytes 6684672 | tf_op jit(solution)/shard_map/all_gather | solution.py:38
  10.0 165.9 %reduce-scatter.4.cloned.1.call-start = ((), (), s32[]{:S(2)}) async-start(), calls=%async_computation.3 | async-start | bytes 6684672
  11.3 49.4 %copy-start = (f32[3,512,512]{2,1,0:T(8,128)S(1)}, f32[3,512,512]{2,1,0:T(8,128)}, u32[]{:S(2)}) copy-start(f32[3,512,512]{2,1,0:T(8,128)} %param.8) | copy-start | bytes 9437188
  60.7 8.3 %copy-start.5 = (f32[3,512,1024]{2,1,0:T(8,128)S(1)}, f32[3,512,1024]{2,1,0:T(8,128)}, u32[]{:S(2)}) copy-start(f32[3,512,1024]{2,1,0:T(8,128)} %all-gather.2.cloned.1.call-done) | copy-start | bytes 18874372
  65.0 8.0 %copy-start.6 = (f32[512,1024]{1,0:T(8,128)}, f32[512,1024]{1,0:T(8,128)S(1)}, u32[]{:S(2)}) copy-start(f32[512,1024]{1,0:T(8,128)S(1)} %bitcast_add_fusion) | copy-start | bytes 6291460
  65.0 4.0 %copy-start.1 = (f32[512,512]{0,1:T(8,128)S(1)}, f32[512,512]{0,1:T(8,128)}, u32[]{:S(2)}) copy-start(f32[512,512]{0,1:T(8,128)} %convolution_subtract_fusion) | copy-start | bytes 3145732
  73.0 16.0 %copy-start.3 = (f32[512,1024]{1,0:T(8,128)}, f32[512,1024]{1,0:T(8,128)S(1)}, u32[]{:S(2)}) copy-start(f32[512,1024]{1,0:T(8,128)S(1)} %fusion.7) | copy-start | bytes 6291460
  92.3 227.9 %all-reduce.3.cloned.1.call-start = ((), (), s32[]{:S(2)}) async-start(), calls=%async_computation.2 | async-start | bytes 786432 | tf_op jit(solution)/shard_map/psum | solution.py:54
  92.4 3.2 copy-start.2
  175.8 11.1 %collective-permute-start = (f32[3,32,1024]{2,1,0:T(8,128)}, f32[3,32,1024]{2,1,0:T(8,128)S(1)}, u32[]{:S(2)}, u32[]{:S(2)}) collective-permute-start(f32[3,32,1024]{2,1,0:T(8,128)} %bitcast.108), channel_id=1, source_target_pairs={{0,0},{1,16},{2,32},{3,48},{4,64},{5,80},{6,96},{7,112},{8,128},{9... | collective-permute-start | bytes 1179656 | tf_op jit(solution)/shard_map/ppermute | solution.py:50
  183.1 4.6 %copy-start.4 = (f32[512,1024]{1,0:T(8,128)S(1)}, f32[512,1024]{1,0:T(8,128)}, u32[]{:S(2)}) copy-start(f32[512,1024]{1,0:T(8,128)} %copy-done.3) | copy-start | bytes 6291460
  183.1 4.6 %copy-start.7 = (f32[512,1024]{1,0:T(8,128)S(1)}, f32[512,1024]{1,0:T(8,128)}, u32[]{:S(2)}) copy-start(f32[512,1024]{1,0:T(8,128)} %copy-done.6) | copy-start | bytes 6291460
  183.2 5.1 %copy-start.8 = (f32[512,1024]{1,0:T(8,128)S(1)}, f32[512,1024]{1,0:T(8,128)}, u32[]{:S(2)}) copy-start(f32[512,1024]{1,0:T(8,128)} %slice_bitcast_fusion.2) | copy-start | bytes 6291460
Sparse Core Ops, SparseCore 0:
  10.4 50.2 all-gather.1
  92.4 83.3 reduce-scatter.3
  195.2 124.9 all-reduce.2

commit v2 on v1

v2 whole, which is shorter than its diff:
```python
import functools

import jax
import jax.numpy as jnp
from jax import lax
from jax.experimental import pallas as pl
from jax.experimental.pallas import tpu as pltpu
from jax.sharding import PartitionSpec as P

NB = 128
F32 = jnp.float32
BF16 = jnp.bfloat16
MESH = pl.DeviceIdType.MESH
highest = lax.Precision.HIGHEST

NN = (((1,), (0,)), ((), ()))
NT = (((1,), (1,)), ((), ()))


def split(value):
    top = value.astype(BF16)
    return top, (value - top.astype(F32)).astype(BF16)


def dot(left, right, dims=NN):
    return lax.dot_general(left, right, dims, preferred_element_type=F32)


def exact(left, right, dims=NN):
    return lax.dot_general(left, right, dims, precision=highest, preferred_element_type=F32)


def lanes(index, size):
    return pl.ds(pl.multiple_of(index * size, 128), size)


def kernel(
    pan, pat, coup, dinv, ainv, xt_out, xc_out, yd_out,
    G, Hh, Hl, A32, Ah, Al, C32, D32, Ch, Cl, PX,
    RLX, FNX, RLY, FNY, RLX2, FNX2, RLY2, FNY2,
    XS, ZB, XF, IN0, IN1, IN2, RB0, RB1, RB2, OU0, OU1, OU2, VD,
    load_sem, ag_s, ag_r, pf_s, pf_r, rs_s, rs_r, za_s, za_r, xa_s, xa_r, ra_s, ra_r, ga_s, ga_r,
):
    r = lax.axis_index("prow")
    c = lax.axis_index("pcol")
    x, y = r // 4, r % 4
    z, core = c // 2, c % 2
    sends = []

    load_pan = pltpu.make_async_copy(pan, G.at[:, c], load_sem.at[0])
    load_a = pltpu.make_async_copy(ainv, A32, load_sem.at[1])
    load_c = pltpu.make_async_copy(coup, C32, load_sem.at[2])
    load_d = pltpu.make_async_copy(dinv, D32, load_sem.at[3])
    load_pan.start()
    load_a.start()
    load_c.start()
    load_d.start()

    barrier = pltpu.get_barrier_semaphore()

    def greet(o, carry):
        pl.semaphore_signal(barrier, inc=1, device_id={"pcol": (c + o) % 16}, device_id_type=MESH)
        pl.semaphore_signal(barrier, inc=1, device_id={"prow": (r + o) % 16}, device_id_type=MESH)
        return carry

    lax.fori_loop(1, 16, greet, 0)
    pl.semaphore_wait(barrier, 30)

    def remote(src, dst, send, recv, device):
        return pltpu.make_async_remote_copy(
            src_ref=src, dst_ref=dst, send_sem=send, recv_sem=recv, device_id=device, device_id_type=MESH
        )

    def start(copy):
        copy.start()
        sends.append(copy)

    def ag(d, k, e, t):
        chip = (z + 8 - t) % 8 if d == 0 else (z + t) % 8
        near = (z + 1) % 8 if d == 0 else (z + 7) % 8
        part = G.at[k, 2 * chip + core, pl.ds(16 * e, 16)]
        return remote(part, part, ag_s.at[d, k, e, t], ag_r.at[d, k, e, t], {"pcol": 2 * near + core})

    def pf(k, e, q):
        part = G.at[k, 2 * ((z + 8 - q) % 8) + core, pl.ds(16 * e, 16)]
        return remote(part, part, pf_s.at[k, e, q], pf_r.at[k, e, q], {"pcol": 2 * z + 1 - core})

    def travels(d, e, t):
        return t < 3 or (t == 3 and d == e)

    def ag_start(k):
        for e in range(2):
            for d in range(2):
                start(ag(d, k, e, 0))
        for e in range(2):
            start(pf(k, e, 0))

    def ag_step(k, t):
        for e in range(2):
            for d in range(2):
                if travels(d, e, t):
                    ag(d, k, e, t).wait_recv()
                    if travels(d, e, t + 1):
                        start(ag(d, k, e, t + 1))
                    start(pf(k, e, t + 1 if d == 0 else 7 - t))

    def ag_end(k):
        for e in range(2):
            for q in range(8):
                pf(k, e, q).wait_recv()

    def prep_a(part):
        def body(i, carry):
            rows = pl.ds(pl.multiple_of(i * 64, 64), 64)
            top, low = split(-A32[rows, :])
            Ah[rows, :] = top
            Al[rows, :] = low
            return carry

        lax.fori_loop(4 * part, 4 * part + 4, body, 0)

    def prep_c():
        def body(i, carry):
            for m in range(3):
                top, low = split(jnp.transpose(C32[m, :, lanes(i, 128)]))
                rows = pl.ds(pl.multiple_of(i * 128, 128), 128)
                Ch[m, rows, :] = top
                Cl[m, rows, :] = low
            return carry

        lax.fori_loop(0, 4, body, 0)

    def prep_d():
        own = pl.ds(pl.multiple_of(c * 32, 32), 32)
        row = lax.broadcasted_iota(jnp.int32, (32, 512), 0) + c * 32
        pick = (lax.broadcasted_iota(jnp.int32, (32, 512), 1) == row).astype(F32)
        c0p = exact(pick, C32[0], NT)
        c1p = exact(pick, C32[1], NT)
        c2p = exact(pick, C32[2], NT)
        d0, d1, d2 = D32[0, own, :], D32[1, own, :], D32[2, own, :]
        u02p = exact(c2p, C32[0], NT) - c1p
        ta = exact(jnp.concatenate([-c0p, u02p], 0), D32[0])
        t0 = jnp.concatenate([d0, ta], 0)
        t1 = exact(-c2p, D32[1])
        zero = jnp.zeros_like(d0)
        v1 = jnp.concatenate([zero, d1, t1], 0) - exact(t0, C32[0])
        v2 = jnp.concatenate([zero, zero, d2], 0) - exact(t0, C32[1]) - exact(v1, C32[2])
        VD[0] = d0
        VD[1] = v1[0:32]
        VD[2] = v2[0:32]
        VD[3] = v1[32:64]
        VD[4] = v2[32:64]
        VD[5] = v2[64:96]

    def comp_h(k):
        def body(j, carry):
            here = lanes(j, 256)
            first = pat[k, r * 8 + 2 * j].astype(F32)
            second = pat[k, r * 8 + 2 * j + 1].astype(F32)
            mask = jnp.where(lax.broadcasted_iota(jnp.int32, (1, 256), 1) < 128, first, second)
            value = G[k, :, :, here].reshape(512, 256) * mask
            for l in range(k):
                m = l if k == 1 else l + 1
                value = value - (
                    dot(Ch[m], Hh[l, :, here]) + dot(Cl[m], Hh[l, :, here]) + dot(Ch[m], Hl[l, :, here])
                )
            top, low = split(value)
            Hh[k, :, here] = top
            Hl[k, :, here] = low
            return carry

        lax.fori_loop(0, 4, body, 0)

    def comp_p(k, lo, hi):
        def body(j, carry):
            here = lanes(j, 256)
            value = dot(Hh[k], Ah[:, here]) + dot(Hh[k], Al[:, here]) + dot(Hl[k], Ah[:, here])
            PX[k, :, :, :, here] = value.reshape(16, 4, 8, 256)
            return carry

        lax.fori_loop(lo, hi, body, 0)

    class Ring:
        def __init__(self, k, phase, own, relay, final, me, device, out):
            self.own, self.relay, self.final, self.me, self.out = own, relay, final, me, out
            right, left = device((me + 1) % 4), device((me + 3) % 4)
            self.next, self.prev, self.far = (me + 1) % 4, (me + 3) % 4, (me + 2) % 4
            lower, upper = pl.ds(0, 4), pl.ds(4, 4)
            sem = lambda i: (rs_s.at[k, phase, i], rs_r.at[k, phase, i])
            self.relay_r = remote(own(self.far, 0), relay.at[0], *sem(0), right)
            self.relay_l = remote(own(self.far, 1), relay.at[1], *sem(1), left)
            self.raw_r = remote(own(self.next, 1), final.at[0, upper], *sem(2), right)
            self.raw_l = remote(own(self.prev, 0), final.at[1, lower], *sem(3), left)
            self.sum_r = remote(relay.at[0], final.at[0, lower], *sem(4), right)
            self.sum_l = remote(relay.at[1], final.at[1, upper], *sem(5), left)

        def start(self):
            for copy in (self.relay_r, self.relay_l, self.raw_r, self.raw_l):
                start(copy)

        def mid(self):
            for side, copy, chunk, onward in (
                (0, self.relay_r, self.next, self.sum_r),
                (1, self.relay_l, self.prev, self.sum_l),
            ):
                copy.wait_recv()
                mine = self.own(chunk, side)

                def body(i, carry):
                    self.relay[side, i] = self.relay[side, i] + mine[i]
                    return carry

                lax.fori_loop(0, 4, body, 0)
                start(onward)

        def end(self):
            for copy in (self.raw_r, self.raw_l, self.sum_r, self.sum_l):
                copy.wait_recv()
            for side in range(2):
                mine = self.own(self.me, side)
                into = self.out(side)

                def body(i, carry):
                    into[i] = mine[i] + self.final[0, 4 * side + i] + self.final[1, 4 * side + i]
                    return carry

                lax.fori_loop(0, 4, body, 0)

    along_x = lambda t: {"prow": t * 4 + y}
    along_y = lambda t: {"prow": x * 4 + t}

    def rings(k):
        def parts(base, h):
            return pl.ds(base + 4 * h, 4)

        own_x1 = lambda t, h: PX.at[k, parts(0, h), t]
        own_y1 = lambda t, h: PX.at[k, parts(8, h), :, :, lanes(t, 256)]
        own_x2 = lambda t, h: PX.at[k, parts(0, h), x, :, lanes(t, 256)]
        own_y2 = lambda t, h: PX.at[k, parts(8, h), t, :, lanes(y, 256)]
        first = (
            Ring(k, 0, own_x1, RLX.at[k], FNX.at[k], x, along_x, lambda h: own_x1(x, h)),
            Ring(k, 1, own_y1, RLY.at[k], FNY.at[k], y, along_y, lambda h: own_y1(y, h)),
        )
        second = (
            Ring(k, 2, own_x2, RLX2.at[k], FNX2.at[k], y, along_y, lambda h: XS.at[parts(0, h), k]),
            Ring(k, 3, own_y2, RLY2.at[k], FNY2.at[k], x, along_x, lambda h: XS.at[parts(8, h), k]),
        )
        return first, second

    ring = [rings(k) for k in range(3)]

    def rs_start(k, phase):
        for item in ring[k][phase]:
            item.start()

    def rs_mid(k, phase):
        for item in ring[k][phase]:
            item.mid()

    def rs_end(k, phase):
        for item in ring[k][phase]:
            item.end()

    def each(copy, action):
        def body(o, carry):
            getattr(copy(o), action)()
            return carry

        lax.fori_loop(1, 16, body, 0)

    loops = []

    def begin(copy):
        each(copy, "start")
        loops.append(copy)

    def za(k):
        def copy(o):
            to = (c + o) % 16
            return remote(XS.at[to, k], ZB.at[c, k], za_s.at[k, o], za_r.at[k, o], {"pcol": to})

        return copy

    def xa(k):
        def copy(o):
            to = (r + o) % 16
            return remote(
                ZB.at[to, k], XF.at[k, x, :, lanes(y, 256)], xa_s.at[k, o], xa_r.at[k, o], {"prow": to}
            )

        return copy

    def za_start(k):
        begin(za(k))
        ZB[c, k] = XS[c, k]

    def xa_start(k):
        each(za(k), "wait_recv")
        begin(xa(k))
        XF[k, x, :, lanes(y, 256)] = ZB[r, k]

    def xa_end(k):
        each(xa(k), "wait_recv")

    IN, RB, OU = (IN0, IN1, IN2), (RB0, RB1, RB2), (OU0, OU1, OU2)

    def inner(k):
        value = XF[k].reshape(32, 1024)
        xt_out[k] = value
        top, low = split(value)
        both = jnp.concatenate([top, low], 0)
        for m in range(k, 3):
            wide = dot(both, Hh[m], NT)
            total = wide[0:32] + wide[32:64] + dot(top, Hl[m], NT)
            IN[k][:, :, pl.ds((m - k) * 512, 512)] = total.reshape(4, 8, 512)

    def ra(k):
        w = 128 * (3 - k)

        def copy(o):
            to = (r + o) % 16
            return remote(
                IN[k].at[to // 4, :, lanes(to % 4, w)], RB[k].at[o], ra_s.at[k, o], ra_r.at[k, o], {"prow": to}
            )

        return copy

    def ga(k):
        w = 128 * (3 - k)
        mine = OU[k].at[x, :, lanes(y, w)]

        def copy(o):
            return remote(mine, mine, ga_s.at[k, o], ga_r.at[k, o], {"prow": (r + o) % 16})

        return copy

    def ar_start(k):
        inner(k)
        begin(ra(k))

    def ar_mid(k):
        w = 128 * (3 - k)
        each(ra(k), "wait_recv")
        total = IN[k][x, :, lanes(y, w)]
        for o in range(1, 16):
            total = total + RB[k][o]
        OU[k][x, :, lanes(y, w)] = total
        begin(ga(k))

    def ar_end(k):
        each(ga(k), "wait_recv")
        places = (((yd_out, 0), (xc_out, 0), (xc_out, 1)), ((yd_out, 1), (xc_out, 2)), ((yd_out, 2),))[k]
        first = (0, 3, 5)[k]
        for i, (target, slot) in enumerate(places):
            got = OU[k][:, :, pl.ds(i * 512, 512)].reshape(32, 512)
            target[slot] = VD[first + i] - got

    load_pan.wait()
    ag_start(0)
    load_a.wait()
    prep_a(0)
    prep_a(1)
    ag_step(0, 0)
    prep_a(2)
    prep_a(3)
    ag_step(0, 1)
    load_c.wait()
    prep_c()
    ag_step(0, 2)
    ag_start(1)
    ag_step(0, 3)
    ag_end(0)
    comp_h(0)
    ag_step(1, 0)
    comp_p(0, 0, 2)
    ag_step(1, 1)
    comp_p(0, 2, 4)
    rs_start(0, 0)
    ag_step(1, 2)
    ag_start(2)
    load_d.wait()
    prep_d()
    ag_step(1, 3)
    rs_mid(0, 0)
    ag_end(1)
    comp_h(1)
    ag_step(2, 0)
    comp_p(1, 0, 2)
    rs_end(0, 0)
    rs_start(0, 1)
    ag_step(2, 1)
    comp_p(1, 2, 4)
    rs_start(1, 0)
    rs_mid(0, 1)
    ag_step(2, 2)
    ag_step(2, 3)
    rs_end(0, 1)
    za_start(0)
    rs_mid(1, 0)
    ag_end(2)
    comp_h(2)
    xa_start(0)
    comp_p(2, 0, 2)
    rs_end(1, 0)
    rs_start(1, 1)
    xa_end(0)
    ar_start(0)
    comp_p(2, 2, 4)
    rs_start(2, 0)
    rs_mid(1, 1)
    ar_mid(0)
    rs_end(1, 1)
    za_start(1)
    rs_mid(2, 0)
    xa_start(1)
    ar_end(0)
    xa_end(1)
    ar_start(1)
    rs_end(2, 0)
    rs_start(2, 1)
    ar_mid(1)
    rs_mid(2, 1)
    rs_end(2, 1)
    za_start(2)
    ar_end(1)
    xa_start(2)
    xa_end(2)
    ar_start(2)
    ar_mid(2)
    ar_end(2)

    for copy in sends:
        copy.wait_send()
    for copy in loops:
        each(copy, "wait_send")


def scratch():
    v = pltpu.VMEM
    sem = pltpu.SemaphoreType.DMA
    return [
        v((3, 16, 32, 1024), F32), v((3, 512, 1024), BF16), v((3, 512, 1024), BF16),
        v((1024, 1024), F32), v((1024, 1024), BF16), v((1024, 1024), BF16),
        v((3, 512, 512), F32), v((3, 512, 512), F32), v((3, 512, 512), BF16), v((3, 512, 512), BF16),
        v((3, 16, 4, 8, 1024), F32),
        v((3, 2, 4, 8, 1024), F32), v((3, 2, 8, 8, 1024), F32),
        v((3, 2, 4, 4, 8, 256), F32), v((3, 2, 8, 4, 8, 256), F32),
        v((3, 2, 4, 8, 256), F32), v((3, 2, 8, 8, 256), F32),
        v((3, 2, 4, 8, 256), F32), v((3, 2, 8, 8, 256), F32),
        v((16, 3, 8, 256), F32), v((16, 3, 8, 256), F32), v((3, 4, 8, 1024), F32),
        v((4, 8, 1536), F32), v((4, 8, 1024), F32), v((4, 8, 512), F32),
        v((16, 8, 384), F32), v((16, 8, 256), F32), v((16, 8, 128), F32),
        v((4, 8, 1536), F32), v((4, 8, 1024), F32), v((4, 8, 512), F32),
        v((6, 32, 512), F32),
        sem((4,)), sem((2, 3, 2, 4)), sem((2, 3, 2, 4)), sem((3, 2, 8)), sem((3, 2, 8)),
        sem((3, 4, 6)), sem((3, 4, 6)),
        sem((3, 16)), sem((3, 16)), sem((3, 16)), sem((3, 16)),
        sem((3, 16)), sem((3, 16)), sem((3, 16)), sem((3, 16)),
    ]


def shards(ainv, panels, pattern, coupling, dinv):
    any_space = pl.BlockSpec(memory_space=pl.ANY)
    vmem = pl.BlockSpec(memory_space=pltpu.VMEM)
    xt, xc, yd = pl.pallas_call(
        kernel,
        out_shape=(
            jax.ShapeDtypeStruct((3, 32, 1024), F32),
            jax.ShapeDtypeStruct((3, 32, 512), F32),
            jax.ShapeDtypeStruct((3, 32, 512), F32),
        ),
        in_specs=[any_space, pl.BlockSpec(memory_space=pltpu.SMEM), any_space, any_space, any_space],
        out_specs=(vmem, vmem, vmem),
        scratch_shapes=scratch(),
        compiler_params=pltpu.CompilerParams(
            collective_id=0, has_side_effects=True, vmem_limit_bytes=64 * 1024 * 1024 - 65536
        ),
    )(jnp.swapaxes(panels, 1, 2), pattern, coupling, dinv, ainv)
    return jnp.swapaxes(xt, 1, 2), xc, yd


def solution(mesh):
    placed = (P("prow", "pcol"), P(None, "prow", "pcol"), P(), P(), P())
    return jax.shard_map(
        shards,
        mesh=mesh,
        in_specs=placed,
        out_specs=(P(None, "prow", "pcol"), P(None, "pcol", None), P(None, "pcol", None)),
        check_vma=False,
    )
```

time: 338 us -> 146 us (0.43)
  waiting for transfers between devices: 245 us -> 0 us
  Pallas kernels: 0 us -> 140 us
  matrix products: 53.1 us -> 0 us
  between operations: 14 us -> 0.64 us
  local copies, waits for them, and re-layouts: 12.9 us -> 5 us
  other arithmetic: 7.1 us -> 0 us
  starting transfers between devices: 5.43 us -> 0 us
    pallas_call x0 -> x1, Pallas kernels: none -> 140 us  [shards(): pl.pallas_call(kernel, out_shape=(jax.ShapeDtypeStruct((3, 32, 1024), F32...]
    psum x1 -> x0, waiting for transfers between devices: 121 us -> none  [shards(): summed = lax.psum(jnp.concatenate([inner0, inner1, inner2], 1), 'prow')]
    unnamed x4 -> x0, waiting for transfers between devices: 79.2 us -> none
    dot_general x18 -> x0, matrix products: 53.1 us -> none  [the longest x9 32.8 us: mm(): jnp.dot(left, right, precision=precision, preferred_element_type=jnp.floa...]
    all_gather x1 -> x0, waiting for transfers between devices: 44.5 us -> none  [shards(): f0, f1, f2 = lax.all_gather(factors, 'pcol', axis=1, tiled=True)]
    ppermute x1 -> x0, starting transfers between devices: 5.31 us -> none  [shards(): xt = -lax.ppermute(mine, ('prow', 'pcol'), perm)]
    another operation x1 -> x0, local copies, waits for them, and re-layouts: 3.98 us -> none  [shards(): f0, f1, f2 = lax.all_gather(factors, 'pcol', axis=1, tiled=True)]
    slice x3 -> x0, local copies, waits for them, and re-layouts: 3.75 us -> none  [the longest x1 3.74 us: shards(): dinv[2]]
  transfers between devices with their start and end apart: 4 -> 0, of which waited for: 3 -> 0; matrix products, arithmetic and copies ran while one was open for 6% -> 0% of each run, Pallas kernels for 0% -> 0%
where the time goes in v2:
time: 146 us
  Pallas kernels  140 us (96%)
  local copies, waits for them, and re-layouts  5 us (3%)
    pallas_call x1, Pallas kernels, shards(): pl.pallas_call(kernel, out_shape=(jax.ShapeDtypeStruct((3, 32, 1024), F32...  140 us
    unnamed x3, local copies, waits for them, and re-layouts  5 us

profile of v2, /device:TPU:1, one launch (start us, length us, event | category | flops | bytes accessed | tf_op | source)
XLA Modules:
  0.0 145.6 jit_solution(16024451411033505208)
XLA Ops:
  0.6 140.0 %shard_map.76 = (f32[3,32,1024]{2,1,0:T(8,128)}, f32[3,32,512]{2,1,0:T(8,128)}, f32[3,32,512]{2,1,0:T(8,128)}) custom-call(f32[3,32,1024]{2,1,0:T(8,128)} %bitcast.2, s32[3,128]{1,0:T(4,128)} %pat.1, f32[3,512,512]{2,1,0:T(8,128)} %coup.1, f32[3,512,512]{2,1,0:T(8,128)} %dinv.1, f32[1024,1024]{1,0:T(8,128)} %ainv.1), custom_call_target="tpu_custom_call" | custom-call | tf_op jit(solution)/shard_map/pallas_call | solution.py:465
  140.6 1.8 %copy.11 = f32[3,1024,32]{1,2,0:T(8,128)} copy(f32[3,1024,32]{1,2,0:T(8,128)} %bitcast.3) | data formatting | bytes 786432
  142.4 1.6 %copy.12 = f32[3,32,512]{2,1,0:T(8,128)} copy(f32[3,32,512]{2,1,0:T(8,128)} %get-tuple-element.13) | data formatting | bytes 393216
  144.0 1.6 %copy.13 = f32[3,32,512]{2,1,0:T(8,128)} copy(f32[3,32,512]{2,1,0:T(8,128)} %get-tuple-element.14) | data formatting | bytes 393216

commit v3 on v2

v3 whole, which is shorter than its diff:
```python
import jax
import jax.numpy as jnp
from jax import lax
from jax.experimental import pallas as pl
from jax.experimental.pallas import tpu as pltpu
from jax.sharding import PartitionSpec as P

NB = 128
F32 = jnp.float32
BF16 = jnp.bfloat16
MESH = pl.DeviceIdType.MESH

NN = (((1,), (0,)), ((), ()))
NT = (((1,), (1,)), ((), ()))


def split(value):
    top = value.astype(BF16)
    return top, (value - top.astype(F32)).astype(BF16)


def dot(left, right, dims=NN):
    return lax.dot_general(left, right, dims, preferred_element_type=F32)


def lanes(index, size):
    return pl.ds(pl.multiple_of(index * size, 128), size)


def kernel(
    pan, pat, coup, dinv, ainv, xt_out, xc_out, yd_out,
    G, Hh, Hl, A32, Ah, Al, C32, D32, Ch, Cl, RM, PX,
    RLX, FNX, RLY, FNY, RLX2, FNX2, RLY2, FNY2,
    XS, ZB, XF, IN0, IN1, IN2, RB0, RB1, RB2, OU0, OU1, OU2, VD,
    load_sem, ag_r, pf_r, rs_r, za_r, xa_r, ra_r, ga_r, sent,
):
    r = lax.axis_index("prow")
    c = lax.axis_index("pcol")
    x, y = r // 4, r % 4
    z, core = c // 2, c % 2

    load_pan = pltpu.make_async_copy(pan, G.at[:, c], load_sem.at[0])
    load_a = pltpu.make_async_copy(ainv, A32, load_sem.at[1])
    load_c = pltpu.make_async_copy(coup, C32, load_sem.at[2])
    load_d = pltpu.make_async_copy(dinv, D32, load_sem.at[3])
    load_pan.start()
    load_a.start()
    load_c.start()
    load_d.start()

    barrier = pltpu.get_barrier_semaphore()

    for near in (2 * ((z + 1) % 8) + core, 2 * ((z + 7) % 8) + core, 2 * z + 1 - core):
        pl.semaphore_signal(barrier, inc=1, device_id={"pcol": near}, device_id_type=MESH)
    for near in (x * 4 + (y + 1) % 4, x * 4 + (y + 3) % 4, (x + 1) % 4 * 4 + y, (x + 3) % 4 * 4 + y):
        pl.semaphore_signal(barrier, inc=1, device_id={"prow": near}, device_id_type=MESH)
    pl.semaphore_wait(barrier, 7)

    def remote(src, dst, send, recv, device):
        return pltpu.make_async_remote_copy(
            src_ref=src, dst_ref=dst, send_sem=send, recv_sem=recv, device_id=device, device_id_type=MESH
        )

    def take(ref, semaphore):
        pltpu.make_async_copy(ref, ref, semaphore).wait()

    def ag(d, k, e, t):
        chip = (z + 8 - t) % 8 if d == 0 else (z + t) % 8
        near = (z + 1) % 8 if d == 0 else (z + 7) % 8
        part = G.at[k, 2 * chip + core, pl.ds(8 * e, 8)]
        return remote(part, part, sent.at[0], ag_r.at[d, k, e, t], {"pcol": 2 * near + core})

    def pf(k, e, q):
        part = G.at[k, 2 * ((z + 8 - q) % 8) + core, pl.ds(8 * e, 8)]
        return remote(part, part, sent.at[1], pf_r.at[k], {"pcol": 2 * z + 1 - core})

    def travels(d, e, t):
        return t < 3 or (t == 3 and d == e // 2)

    def ag_start(k):
        for e in range(4):
            for d in range(2):
                ag(d, k, e, 0).start()
        for e in range(4):
            pf(k, e, 0).start()

    def ag_step(k, t):
        for e in range(4):
            for d in range(2):
                if travels(d, e, t):
                    ag(d, k, e, t).wait_recv()
                    if travels(d, e, t + 1):
                        ag(d, k, e, t + 1).start()
                    pf(k, e, t + 1 if d == 0 else 7 - t).start()

    def ag_end(k):
        take(G.at[k, pl.ds(0, 8)], pf_r.at[k])

    def prep_a(part):
        def body(i, carry):
            rows = pl.ds(pl.multiple_of(i * 64, 64), 64)
            top, low = split(-A32[rows, :])
            Ah[rows, :] = top
            Al[rows, :] = low
            return carry

        lax.fori_loop(4 * part, 4 * part + 4, body, 0)

    def prep_c():
        def body(i, carry):
            for m in range(3):
                top, low = split(jnp.transpose(C32[m, :, lanes(i, 128)]))
                rows = pl.ds(pl.multiple_of(i * 128, 128), 128)
                Ch[m, rows, :] = top
                Cl[m, rows, :] = low
            return carry

        lax.fori_loop(0, 4, body, 0)

    def triple(left, top, low, dims=NN):
        n = left.shape[0]
        a, b = split(left)
        wide = dot(jnp.concatenate([a, b], 0), top, dims)
        return wide[0:n] + wide[n:] + dot(a, low, dims)

    def prep_d():
        own = pl.ds(pl.multiple_of(c * 32, 32), 32)
        c0p, c1p, c2p = (Ch[m, own, :].astype(F32) + Cl[m, own, :].astype(F32) for m in range(3))
        d0, d1, d2 = D32[0, own, :], D32[1, own, :], D32[2, own, :]
        u02p = triple(c2p, Ch[0], Cl[0]) - c1p
        t0 = jnp.concatenate([d0, triple(jnp.concatenate([-c0p, u02p], 0), *split(D32[0]))], 0)
        t1 = triple(-c2p, *split(D32[1]))
        zero = jnp.zeros_like(d0)
        v1 = jnp.concatenate([zero, d1, t1], 0) - triple(t0, Ch[0], Cl[0], NT)
        v2 = jnp.concatenate([zero, zero, d2], 0) - triple(t0, Ch[1], Cl[1], NT) - triple(v1, Ch[2], Cl[2], NT)
        VD[0] = d0
        VD[1] = v1[0:32]
        VD[2] = v2[0:32]
        VD[3] = v1[32:64]
        VD[4] = v2[32:64]
        VD[5] = v2[64:96]

    def comp_r(k, lo, hi):
        def body(j, carry):
            here = lanes(j, 256)
            value = jnp.zeros((512, 256), F32)
            for l in range(k):
                m = l if k == 1 else l + 1
                value = value + (
                    dot(Ch[m], Hh[l, :, here]) + dot(Cl[m], Hh[l, :, here]) + dot(Ch[m], Hl[l, :, here])
                )
            RM[:, here] = value
            return carry

        lax.fori_loop(lo, hi, body, 0)

    def comp_h(k):
        def body(j, carry):
            here = lanes(j, 256)
            first = pat[k, r * 8 + 2 * j].astype(F32)
            second = pat[k, r * 8 + 2 * j + 1].astype(F32)
            mask = jnp.where(lax.broadcasted_iota(jnp.int32, (1, 256), 1) < 128, first, second)
            value = G[k, :, :, here].reshape(512, 256) * mask
            if k > 0:
                value = value - RM[:, here]
            top, low = split(value)
            Hh[k, :, here] = top
            Hl[k, :, here] = low
            return carry

        lax.fori_loop(0, 4, body, 0)

    def comp_p(k, half):
        rows = pl.ds(256 * half, 256)

        def body(j, carry):
            here = lanes(j, 256)
            top, low = Hh[k, rows, :], Hl[k, rows, :]
            value = dot(top, Ah[:, here]) + dot(low, Ah[:, here]) + dot(top, Al[:, here])
            PX[k, pl.ds(8 * half, 8), :, :, here] = value.reshape(8, 4, 8, 256)
            return carry

        lax.fori_loop(0, 4, body, 0)

    class Ring:
        def __init__(self, k, phase, own, relay, final, me, device, out):
            self.own, self.relay, self.final, self.me, self.out = own, relay, final, me, out
            right, left = device((me + 1) % 4), device((me + 3) % 4)
            self.next, self.prev, self.far = (me + 1) % 4, (me + 3) % 4, (me + 2) % 4
            lower, upper = pl.ds(0, 4), pl.ds(4, 4)
            self.done = rs_r.at[k, phase, 2]
            sem = lambda i: (sent.at[2], rs_r.at[k, phase, i])
            self.relay_r = remote(own(self.far, 0), relay.at[0], *sem(0), right)
            self.relay_l = remote(own(self.far, 1), relay.at[1], *sem(1), left)
            self.raw_r = remote(own(self.next, 1), final.at[0, upper], *sem(2), right)
            self.raw_l = remote(own(self.prev, 0), final.at[1, lower], *sem(2), left)
            self.sum_r = remote(relay.at[0], final.at[0, lower], *sem(2), right)
            self.sum_l = remote(relay.at[1], final.at[1, upper], *sem(2), left)

        def start(self):
            for copy in (self.relay_r, self.relay_l, self.raw_r, self.raw_l):
                copy.start()

        def mid(self):
            for side, copy, chunk, onward in (
                (0, self.relay_r, self.next, self.sum_r),
                (1, self.relay_l, self.prev, self.sum_l),
            ):
                copy.wait_recv()
                mine = self.own(chunk, side)

                def body(i, carry):
                    self.relay[side, i] = self.relay[side, i] + mine[i]
                    return carry

                lax.fori_loop(0, 4, body, 0)
                onward.start()

        def end(self):
            take(self.final, self.done)
            for side in range(2):
                mine = self.own(self.me, side)
                into = self.out(side)

                def body(i, carry):
                    into[i] = mine[i] + self.final[0, 4 * side + i] + self.final[1, 4 * side + i]
                    return carry

                lax.fori_loop(0, 4, body, 0)

    along_x = lambda t: {"prow": t * 4 + y}
    along_y = lambda t: {"prow": x * 4 + t}

    def rings(k):
        def parts(base, h):
            return pl.ds(base + 4 * h, 4)

        own_x1 = lambda t, h: PX.at[k, parts(0, h), t]
        own_y1 = lambda t, h: PX.at[k, parts(8, h), :, :, lanes(t, 256)]
        own_x2 = lambda t, h: PX.at[k, parts(0, h), x, :, lanes(t, 256)]
        own_y2 = lambda t, h: PX.at[k, parts(8, h), t, :, lanes(y, 256)]
        first = (
            Ring(k, 0, own_x1, RLX.at[k], FNX.at[k], x, along_x, lambda h: own_x1(x, h)),
            Ring(k, 1, own_y1, RLY.at[k], FNY.at[k], y, along_y, lambda h: own_y1(y, h)),
        )
        second = (
            Ring(k, 2, own_x2, RLX2.at[k], FNX2.at[k], y, along_y, lambda h: XS.at[parts(0, h), k]),
            Ring(k, 3, own_y2, RLY2.at[k], FNY2.at[k], x, along_x, lambda h: XS.at[parts(8, h), k]),
        )
        return first, second

    ring = [rings(k) for k in range(3)]

    def rs_start(k, phase, *which):
        for i in which or (0, 1):
            ring[k][phase][i].start()

    def rs_mid(k, phase):
        for item in ring[k][phase]:
            item.mid()

    def rs_end(k, phase):
        for item in ring[k][phase]:
            item.end()

    def begin(copy):
        def body(o, carry):
            copy(o).start()
            return carry

        lax.fori_loop(1, 16, body, 0)

    def za(k):
        def copy(o):
            to = (c + o) % 16
            return remote(XS.at[to, k], ZB.at[c, k], sent.at[3], za_r.at[k], {"pcol": to})

        return copy

    def xa(k):
        def copy(o):
            to = (r + o) % 16
            return remote(
                ZB.at[to, k], XF.at[k, x, :, lanes(y, 256)], sent.at[4], xa_r.at[k], {"prow": to}
            )

        return copy

    def za_start(k):
        begin(za(k))
        ZB[c, k] = XS[c, k]

    def xa_start(k):
        take(ZB.at[pl.ds(0, 15), k], za_r.at[k])
        begin(xa(k))
        XF[k, x, :, lanes(y, 256)] = ZB[r, k]

    def xa_end(k):
        take(ZB.at[pl.ds(0, 15), k], xa_r.at[k])

    IN, RB, OU = (IN0, IN1, IN2), (RB0, RB1, RB2), (OU0, OU1, OU2)

    def inner(k):
        value = XF[k].reshape(32, 1024)
        xt_out[k] = value
        top, low = split(value)
        both = jnp.concatenate([top, low], 0)
        for m in range(k, 3):
            wide = dot(both, Hh[m], NT)
            total = wide[0:32] + wide[32:64] + dot(top, Hl[m], NT)
            IN[k][:, :, pl.ds((m - k) * 512, 512)] = total.reshape(4, 8, 512)

    def ra(k):
        w = 128 * (3 - k)

        def copy(o):
            to = (r + o) % 16
            return remote(
                IN[k].at[to // 4, :, lanes(to % 4, w)], RB[k].at[o], sent.at[5], ra_r.at[k], {"prow": to}
            )

        return copy

    def ga(k):
        w = 128 * (3 - k)
        mine = OU[k].at[x, :, lanes(y, w)]

        def copy(o):
            return remote(mine, mine, sent.at[6], ga_r.at[k], {"prow": (r + o) % 16})

        return copy

    def ar_start(k):
        inner(k)
        begin(ra(k))

    def ar_mid(k):
        w = 128 * (3 - k)
        take(RB[k].at[pl.ds(1, 15)], ra_r.at[k])
        total = IN[k][x, :, lanes(y, w)]
        for o in range(1, 16):
            total = total + RB[k][o]
        OU[k][x, :, lanes(y, w)] = total
        begin(ga(k))

    def ar_end(k):
        take(RB[k].at[pl.ds(1, 15)], ga_r.at[k])
        places = (((yd_out, 0), (xc_out, 0), (xc_out, 1)), ((yd_out, 1), (xc_out, 2)), ((yd_out, 2),))[k]
        first = (0, 3, 5)[k]
        for i, (target, slot) in enumerate(places):
            got = OU[k][:, :, pl.ds(i * 512, 512)].reshape(32, 512)
            target[slot] = VD[first + i] - got

    load_pan.wait()
    ag_start(0)
    load_a.wait()
    prep_a(0)
    prep_a(1)
    ag_step(0, 0)
    prep_a(2)
    prep_a(3)
    load_c.wait()
    prep_c()
    ag_step(0, 1)
    load_d.wait()
    prep_d()
    ag_step(0, 2)
    ag_start(1)
    ag_step(0, 3)
    ag_end(0)
    comp_h(0)
    comp_p(0, 0)
    rs_start(0, 0, 0)
    ag_step(1, 0)
    comp_p(0, 1)
    rs_start(0, 0, 1)
    ag_step(1, 1)
    comp_r(1, 0, 4)
    rs_mid(0, 0)
    ag_step(1, 2)
    ag_start(2)
    ag_step(1, 3)
    ag_end(1)
    comp_h(1)
    comp_p(1, 0)
    rs_end(0, 0)
    rs_start(0, 1)
    rs_start(1, 0, 0)
    ag_step(2, 0)
    comp_p(1, 1)
    rs_start(1, 0, 1)
    ag_step(2, 1)
    comp_r(2, 0, 2)
    rs_mid(0, 1)
    rs_mid(1, 0)
    ag_step(2, 2)
    comp_r(2, 2, 4)
    ag_step(2, 3)
    rs_end(0, 1)
    za_start(0)
    ag_end(2)
    comp_h(2)
    comp_p(2, 0)
    rs_start(2, 0, 0)
    comp_p(2, 1)
    rs_start(2, 0, 1)
    xa_start(0)
    rs_end(1, 0)
    rs_start(1, 1)
    xa_end(0)
    ar_start(0)
    rs_mid(1, 1)
    rs_mid(2, 0)
    rs_end(1, 1)
    za_start(1)
    ar_mid(0)
    rs_end(2, 0)
    rs_start(2, 1)
    xa_start(1)
    rs_mid(2, 1)
    xa_end(1)
    ar_start(1)
    rs_end(2, 1)
    za_start(2)
    ar_end(0)
    ar_mid(1)
    xa_start(2)
    ar_end(1)
    xa_end(2)
    ar_start(2)
    ar_mid(2)
    ar_end(2)

    for i, ref in enumerate((
        G.at[:, pl.ds(0, 7)], G.at[:, pl.ds(0, 8)], PX.at[:, pl.ds(0, 15)],
        ZB.at[pl.ds(0, 15)], ZB.at[pl.ds(0, 15)], ZB.at[pl.ds(0, 15)], ZB.at[pl.ds(0, 15)],
    )):
        take(ref, sent.at[i])


def finish(xt, xc, yd, xt_out, xc_out, yd_out, a, b, c, inward, outward):
    trips = []
    for i, (source, held, target) in enumerate(((xt, a, xt_out), (xc, b, xc_out), (yd, c, yd_out))):
        arrive = pltpu.make_async_copy(source, held, inward.at[i])
        arrive.start()
        trips.append((arrive, pltpu.make_async_copy(held, target, outward.at[i])))
    for arrive, leave in trips:
        arrive.wait()
        leave.start()
    for arrive, leave in trips:
        leave.wait()


def scratch():
    v = pltpu.VMEM
    sem = pltpu.SemaphoreType.DMA
    return [
        v((3, 16, 32, 1024), F32), v((3, 512, 1024), BF16), v((3, 512, 1024), BF16),
        v((1024, 1024), F32), v((1024, 1024), BF16), v((1024, 1024), BF16),
        v((3, 512, 512), F32), v((3, 512, 512), F32), v((3, 512, 512), BF16), v((3, 512, 512), BF16),
        v((512, 1024), F32),
        v((3, 16, 4, 8, 1024), F32),
        v((3, 2, 4, 8, 1024), F32), v((3, 2, 8, 8, 1024), F32),
        v((3, 2, 4, 4, 8, 256), F32), v((3, 2, 8, 4, 8, 256), F32),
        v((3, 2, 4, 8, 256), F32), v((3, 2, 8, 8, 256), F32),
        v((3, 2, 4, 8, 256), F32), v((3, 2, 8, 8, 256), F32),
        v((16, 3, 8, 256), F32), v((16, 3, 8, 256), F32), v((3, 4, 8, 1024), F32),
        v((4, 8, 1536), F32), v((4, 8, 1024), F32), v((4, 8, 512), F32),
        v((16, 8, 384), F32), v((16, 8, 256), F32), v((16, 8, 128), F32),
        v((4, 8, 1536), F32), v((4, 8, 1024), F32), v((4, 8, 512), F32),
        v((6, 32, 512), F32),
        sem((4,)), sem((2, 3, 4, 4)), sem((3,)), sem((3, 4, 3)),
        sem((3,)), sem((3,)), sem((3,)), sem((3,)), sem((7,)),
    ]


def shards(ainv, panels, pattern, coupling, dinv):
    any_space = pl.BlockSpec(memory_space=pl.ANY)
    vmem = pl.BlockSpec(memory_space=pltpu.VMEM)
    shapes = ((3, 32, 1024), (3, 32, 512), (3, 32, 512))
    results = tuple(jax.ShapeDtypeStruct(shape, F32) for shape in shapes)
    held = pl.pallas_call(
        kernel,
        out_shape=results,
        in_specs=[any_space, pl.BlockSpec(memory_space=pltpu.SMEM), any_space, any_space, any_space],
        out_specs=(vmem, vmem, vmem),
        scratch_shapes=scratch(),
        compiler_params=pltpu.CompilerParams(
            collective_id=0, has_side_effects=True, vmem_limit_bytes=64 * 1024 * 1024 - 65536
        ),
    )(jnp.swapaxes(panels, 1, 2), pattern, coupling, dinv, ainv)
    xt, xc, yd = pl.pallas_call(
        finish,
        out_shape=results,
        in_specs=[any_space] * 3,
        out_specs=(any_space,) * 3,
        scratch_shapes=[pltpu.VMEM(shape, F32) for shape in shapes] + [pltpu.SemaphoreType.DMA((3,))] * 2,
    )(*held)
    return jnp.swapaxes(xt, 1, 2), xc, yd


def solution(mesh):
    placed = (P("prow", "pcol"), P(None, "prow", "pcol"), P(), P(), P())
    return jax.shard_map(
        shards,
        mesh=mesh,
        in_specs=placed,
        out_specs=(P(None, "prow", "pcol"), P(None, "pcol", None), P(None, "pcol", None)),
        check_vma=False,
    )
```

time: 146 us -> 120 us (0.82)
  Pallas kernels: 140 us -> 118 us
  local copies, waits for them, and re-layouts: 5 us -> 0 us
    pallas_call x1 -> x2, Pallas kernels: 140 us -> 118 us  [the longest x1 116 us: shards(): pl.pallas_call(kernel, out_shape=results, in_specs=[any_space, pl.BlockSp...]
    unnamed x3 -> x0, local copies, waits for them, and re-layouts: 5 us -> none
where the time goes in v3:
time: 120 us; the launch traced here: 119 us
  Pallas kernels  118 us (98%)
    pallas_call x1, Pallas kernels, shards(): pl.pallas_call(kernel, out_shape=results, in_specs=[any_space, pl.BlockSp...  116 us

profile of v3, /device:TPU:1, one launch (start us, length us, event | category | flops | bytes accessed | tf_op | source)
XLA Modules:
  0.0 118.7 jit_solution(1795134036556974030)
XLA Ops:
  0.6 116.1 %shard_map.76 = (f32[3,32,1024]{2,1,0:T(8,128)}, f32[3,32,512]{2,1,0:T(8,128)}, f32[3,32,512]{2,1,0:T(8,128)}) custom-call(f32[3,32,1024]{2,1,0:T(8,128)} %bitcast.2, s32[3,128]{1,0:T(4,128)} %pat.1, f32[3,512,512]{2,1,0:T(8,128)} %coup.1, f32[3,512,512]{2,1,0:T(8,128)} %dinv.1, f32[1024,1024]{1,0:T(8,128)} %ainv.1), custom_call_target="tpu_custom_call" | custom-call | tf_op jit(solution)/shard_map/pallas_call | solution.py:482
  116.8 1.9 %shard_map.77 = (f32[3,32,1024]{2,1,0:T(8,128)}, f32[3,32,512]{2,1,0:T(8,128)}, f32[3,32,512]{2,1,0:T(8,128)}) custom-call(f32[3,32,1024]{2,1,0:T(8,128)} %get-tuple-element.9.xt, f32[3,32,512]{2,1,0:T(8,128)} %get-tuple-element.10.xc, f32[3,32,512]{2,1,0:T(8,128)} %get-tuple-element.11.yd), custom_call_target="tpu_custom_call" | custom-call | tf_op jit(solution)/shard_map/pallas_call | solution.py:492

commit v4 on v3

--- a/solution.py
+++ b/solution.py
@@ -29,7 +29,7 @@
 
 def kernel(
     pan, pat, coup, dinv, ainv, xt_out, xc_out, yd_out,
-    G, Hh, Hl, A32, Ah, Al, C32, D32, Ch, Cl, RM, PX,
+    G, HS, A32, Ah, Al, C32, D32, Ch, Cl, RM, PX,
     RLX, FNX, RLY, FNY, RLX2, FNX2, RLY2, FNY2,
     XS, ZB, XF, IN0, IN1, IN2, RB0, RB1, RB2, OU0, OU1, OU2, VD,
     load_sem, ag_r, pf_r, rs_r, za_r, xa_r, ra_r, ga_r, sent,
@@ -89,9 +89,9 @@
             for d in range(2):
                 if travels(d, e, t):
                     ag(d, k, e, t).wait_recv()
+                    pf(k, e, t + 1 if d == 0 else 7 - t).start()
                     if travels(d, e, t + 1):
                         ag(d, k, e, t + 1).start()
-                    pf(k, e, t + 1 if d == 0 else 7 - t).start()
 
     def ag_end(k):
         take(G.at[k, pl.ds(0, 8)], pf_r.at[k])
@@ -146,9 +146,11 @@
             value = jnp.zeros((512, 256), F32)
             for l in range(k):
                 m = l if k == 1 else l + 1
-                value = value + (
-                    dot(Ch[m], Hh[l, :, here]) + dot(Cl[m], Hh[l, :, here]) + dot(Ch[m], Hl[l, :, here])
-                )
+                for h in range(2):
+                    deep = pl.ds(256 * h, 256)
+                    top, low = HS[l, h, pl.ds(0, 256), here], HS[l, h, pl.ds(256, 256), here]
+                    left = Ch[m, :, deep]
+                    value = value + (dot(left, top) + dot(Cl[m, :, deep], top) + dot(left, low))
             RM[:, here] = value
             return carry
 
@@ -164,23 +166,33 @@
             if k > 0:
                 value = value - RM[:, here]
             top, low = split(value)
-            Hh[k, :, here] = top
-            Hl[k, :, here] = low
+            for h in range(2):
+                HS[k, h, pl.ds(0, 256), here] = top[256 * h : 256 * h + 256]
+                HS[k, h, pl.ds(256, 256), here] = low[256 * h : 256 * h + 256]
             return carry
 
         lax.fori_loop(0, 4, body, 0)
 
-    def comp_p(k, half):
-        rows = pl.ds(256 * half, 256)
-
+    def comp_all(k, lo, hi):
         def body(j, carry):
             here = lanes(j, 256)
-            top, low = Hh[k, rows, :], Hl[k, rows, :]
-            value = dot(top, Ah[:, here]) + dot(low, Ah[:, here]) + dot(top, Al[:, here])
+            for h in range(2):
+                wide = dot(HS[k, h], Ah[:, here])
+                value = wide[0:256] + wide[256:512] + dot(HS[k, h, pl.ds(0, 256), :], Al[:, here])
+                PX[k, pl.ds(8 * h, 8), :, :, here] = value.reshape(8, 4, 8, 256)
+            return carry
+
+        lax.fori_loop(lo, hi, body, 0)
+
+    def comp_p(k, half, lo, hi):
+        def body(j, carry):
+            here = lanes(j, 256)
+            wide = dot(HS[k, half], Ah[:, here])
+            value = wide[0:256] + wide[256:512] + dot(HS[k, half, pl.ds(0, 256), :], Al[:, here])
             PX[k, pl.ds(8 * half, 8), :, :, here] = value.reshape(8, 4, 8, 256)
             return carry
 
-        lax.fori_loop(0, 4, body, 0)
+        lax.fori_loop(lo, hi, body, 0)
 
     class Ring:
         def __init__(self, k, phase, own, relay, final, me, device, out):
@@ -255,13 +267,13 @@
         for i in which or (0, 1):
             ring[k][phase][i].start()
 
-    def rs_mid(k, phase):
-        for item in ring[k][phase]:
-            item.mid()
-
-    def rs_end(k, phase):
-        for item in ring[k][phase]:
-            item.end()
+    def rs_mid(k, phase, *which):
+        for i in which or (0, 1):
+            ring[k][phase][i].mid()
+
+    def rs_end(k, phase, *which):
+        for i in which or (0, 1):
+            ring[k][phase][i].end()
 
     def begin(copy):
         def body(o, carry):
@@ -306,9 +318,10 @@
         top, low = split(value)
         both = jnp.concatenate([top, low], 0)
         for m in range(k, 3):
-            wide = dot(both, Hh[m], NT)
-            total = wide[0:32] + wide[32:64] + dot(top, Hl[m], NT)
-            IN[k][:, :, pl.ds((m - k) * 512, 512)] = total.reshape(4, 8, 512)
+            for h in range(2):
+                wide = dot(both, HS[m, h, pl.ds(0, 256), :], NT)
+                total = wide[0:32] + wide[32:64] + dot(top, HS[m, h, pl.ds(256, 256), :], NT)
+                IN[k][:, :, pl.ds((m - k) * 512 + 256 * h, 256)] = total.reshape(4, 8, 256)
 
     def ra(k):
         w = 128 * (3 - k)
@@ -362,73 +375,74 @@
     load_c.wait()
     prep_c()
     ag_step(0, 1)
+    ag_start(1)
     load_d.wait()
     prep_d()
     ag_step(0, 2)
-    ag_start(1)
+    ag_step(1, 0)
     ag_step(0, 3)
+    ag_start(2)
     ag_end(0)
     comp_h(0)
-    comp_p(0, 0)
-    rs_start(0, 0, 0)
-    ag_step(1, 0)
-    comp_p(0, 1)
-    rs_start(0, 0, 1)
     ag_step(1, 1)
+    comp_all(0, 0, 2)
+    ag_step(2, 0)
+    comp_all(0, 2, 4)
+    rs_start(0, 0)
+    ag_step(1, 2)
     comp_r(1, 0, 4)
+    ag_step(2, 1)
+    ag_step(1, 3)
     rs_mid(0, 0)
-    ag_step(1, 2)
-    ag_start(2)
-    ag_step(1, 3)
     ag_end(1)
     comp_h(1)
-    comp_p(1, 0)
+    comp_all(1, 0, 2)
+    ag_step(2, 2)
+    comp_all(1, 2, 4)
     rs_end(0, 0)
     rs_start(0, 1)
-    rs_start(1, 0, 0)
-    ag_step(2, 0)
-    comp_p(1, 1)
-    rs_start(1, 0, 1)
-    ag_step(2, 1)
+    rs_start(1, 0)
     comp_r(2, 0, 2)
+    ag_step(2, 3)
     rs_mid(0, 1)
+    comp_r(2, 2, 4)
+    ag_end(2)
+    comp_h(2)
+    comp_p(2, 0, 0, 2)
     rs_mid(1, 0)
-    ag_step(2, 2)
-    comp_r(2, 2, 4)
-    ag_step(2, 3)
+    comp_p(2, 0, 2, 4)
+    rs_start(2, 0, 0)
+    comp_p(2, 1, 0, 4)
+    rs_start(2, 0, 1)
     rs_end(0, 1)
     za_start(0)
-    ag_end(2)
-    comp_h(2)
-    comp_p(2, 0)
-    rs_start(2, 0, 0)
-    comp_p(2, 1)
-    rs_start(2, 0, 1)
-    xa_start(0)
     rs_end(1, 0)
     rs_start(1, 1)
-    xa_end(0)
-    ar_start(0)
+    rs_mid(2, 0)
+    xa_start(0)
     rs_mid(1, 1)
-    rs_mid(2, 0)
+    rs_end(2, 0, 0)
+    rs_start(2, 1, 0)
+    rs_end(2, 0, 1)
+    rs_start(2, 1, 1)
     rs_end(1, 1)
     za_start(1)
-    ar_mid(0)
-    rs_end(2, 0)
-    rs_start(2, 1)
+    rs_mid(2, 1)
+    xa_end(0)
+    rs_end(2, 1)
+    za_start(2)
+    ar_start(0)
     xa_start(1)
-    rs_mid(2, 1)
+    xa_start(2)
     xa_end(1)
     ar_start(1)
-    rs_end(2, 1)
-    za_start(2)
-    ar_end(0)
-    ar_mid(1)
-    xa_start(2)
-    ar_end(1)
+    ar_mid(0)
     xa_end(2)
     ar_start(2)
+    ar_mid(1)
+    ar_end(0)
     ar_mid(2)
+    ar_end(1)
     ar_end(2)
 
     for i, ref in enumerate((
@@ -455,7 +469,7 @@
     v = pltpu.VMEM
     sem = pltpu.SemaphoreType.DMA
     return [
-        v((3, 16, 32, 1024), F32), v((3, 512, 1024), BF16), v((3, 512, 1024), BF16),
+        v((3, 16, 32, 1024), F32), v((3, 2, 512, 1024), BF16),
         v((1024, 1024), F32), v((1024, 1024), BF16), v((1024, 1024), BF16),
         v((3, 512, 512), F32), v((3, 512, 512), F32), v((3, 512, 512), BF16), v((3, 512, 512), BF16),
         v((512, 1024), F32),

time: 120 us -> 102 us (0.85)
  Pallas kernels: 118 us -> 101 us
    pallas_call x1, Pallas kernels: 116 us -> 98.9 us  [shards(): pl.pallas_call(kernel, out_shape=results, in_specs=[any_space, pl.BlockSp...]
where the time goes in v4:
time: 102 us; the launch traced here: 101 us
  Pallas kernels  101 us (99%)
    pallas_call x1, Pallas kernels, shards(): pl.pallas_call(kernel, out_shape=results, in_specs=[any_space, pl.BlockSp...  98.9 us

profile of v4, /device:TPU:1, one launch (start us, length us, event | category | flops | bytes accessed | tf_op | source)
XLA Modules:
  0.0 101.5 jit_solution(7619723704732393062)
XLA Ops:
  0.6 98.9 %shard_map.76 = (f32[3,32,1024]{2,1,0:T(8,128)}, f32[3,32,512]{2,1,0:T(8,128)}, f32[3,32,512]{2,1,0:T(8,128)}) custom-call(f32[3,32,1024]{2,1,0:T(8,128)} %bitcast.2, s32[3,128]{1,0:T(4,128)} %pat.1, f32[3,512,512]{2,1,0:T(8,128)} %coup.1, f32[3,512,512]{2,1,0:T(8,128)} %dinv.1, f32[1024,1024]{1,0:T(8,128)} %ainv.1), custom_call_target="tpu_custom_call" | custom-call | tf_op jit(solution)/shard_map/pallas_call | solution.py:496
  99.6 1.9 %shard_map.77 = (f32[3,32,1024]{2,1,0:T(8,128)}, f32[3,32,512]{2,1,0:T(8,128)}, f32[3,32,512]{2,1,0:T(8,128)}) custom-call(f32[3,32,1024]{2,1,0:T(8,128)} %get-tuple-element.9.xt, f32[3,32,512]{2,1,0:T(8,128)} %get-tuple-element.10.xc, f32[3,32,512]{2,1,0:T(8,128)} %get-tuple-element.11.yd), custom_call_target="tpu_custom_call" | custom-call | tf_op jit(solution)/shard_map/pallas_call | solution.py:506

commit v5 on v4

--- a/solution.py
+++ b/solution.py
@@ -29,7 +29,7 @@
 
 def kernel(
     pan, pat, coup, dinv, ainv, xt_out, xc_out, yd_out,
-    G, HS, A32, Ah, Al, C32, D32, Ch, Cl, RM, PX,
+    G, HS, flags, A32, Ah, Al, C32, D32, Ch, Cl, RM, PXX, PYY,
     RLX, FNX, RLY, FNY, RLX2, FNX2, RLY2, FNY2,
     XS, ZB, XF, IN0, IN1, IN2, RB0, RB1, RB2, OU0, OU1, OU2, VD,
     load_sem, ag_r, pf_r, rs_r, za_r, xa_r, ra_r, ga_r, sent,
@@ -43,10 +43,8 @@
     load_a = pltpu.make_async_copy(ainv, A32, load_sem.at[1])
     load_c = pltpu.make_async_copy(coup, C32, load_sem.at[2])
     load_d = pltpu.make_async_copy(dinv, D32, load_sem.at[3])
+    load_f = pltpu.make_async_copy(pat, flags, load_sem.at[4])
     load_pan.start()
-    load_a.start()
-    load_c.start()
-    load_d.start()
 
     barrier = pltpu.get_barrier_semaphore()
 
@@ -140,18 +138,18 @@
         VD[4] = v2[32:64]
         VD[5] = v2[64:96]
 
-    def comp_r(k, lo, hi):
+    def comp_r(k, l, lo, hi):
+        m = k + l - 1
+
         def body(j, carry):
             here = lanes(j, 256)
-            value = jnp.zeros((512, 256), F32)
-            for l in range(k):
-                m = l if k == 1 else l + 1
-                for h in range(2):
-                    deep = pl.ds(256 * h, 256)
-                    top, low = HS[l, h, pl.ds(0, 256), here], HS[l, h, pl.ds(256, 256), here]
-                    left = Ch[m, :, deep]
-                    value = value + (dot(left, top) + dot(Cl[m, :, deep], top) + dot(left, low))
-            RM[:, here] = value
+            value = jnp.zeros((512, 256), F32) if l == 0 else RM[k - 1, :, here]
+            for h in range(2):
+                deep = pl.ds(256 * h, 256)
+                top, low = HS[l, h, pl.ds(0, 256), here], HS[l, h, pl.ds(256, 256), here]
+                left = Ch[m, :, deep]
+                value = value + (dot(left, top) + dot(Cl[m, :, deep], top) + dot(left, low))
+            RM[k - 1, :, here] = value
             return carry
 
         lax.fori_loop(lo, hi, body, 0)
@@ -159,12 +157,12 @@
     def comp_h(k):
         def body(j, carry):
             here = lanes(j, 256)
-            first = pat[k, r * 8 + 2 * j].astype(F32)
-            second = pat[k, r * 8 + 2 * j + 1].astype(F32)
+            first = flags[k, r * 8 + 2 * j].astype(F32)
+            second = flags[k, r * 8 + 2 * j + 1].astype(F32)
             mask = jnp.where(lax.broadcasted_iota(jnp.int32, (1, 256), 1) < 128, first, second)
             value = G[k, :, :, here].reshape(512, 256) * mask
             if k > 0:
-                value = value - RM[:, here]
+                value = value - RM[k - 1, :, here]
             top, low = split(value)
             for h in range(2):
                 HS[k, h, pl.ds(0, 256), here] = top[256 * h : 256 * h + 256]
@@ -173,23 +171,28 @@
 
         lax.fori_loop(0, 4, body, 0)
 
+    def product(k, half, j):
+        here = lanes(j, 256)
+        wide = dot(HS[k, half], Ah[:, here])
+        value = wide[0:256] + wide[256:512] + dot(HS[k, half, pl.ds(0, 256), :], Al[:, here])
+        value = value.reshape(8, 4, 8, 256)
+        if half == 1:
+            PYY[k, j] = value
+        else:
+            for i in range(4):
+                PXX[k, i, :, :, here] = value[:, i]
+
     def comp_all(k, lo, hi):
         def body(j, carry):
-            here = lanes(j, 256)
-            for h in range(2):
-                wide = dot(HS[k, h], Ah[:, here])
-                value = wide[0:256] + wide[256:512] + dot(HS[k, h, pl.ds(0, 256), :], Al[:, here])
-                PX[k, pl.ds(8 * h, 8), :, :, here] = value.reshape(8, 4, 8, 256)
+            product(k, 0, j)
+            product(k, 1, j)
             return carry
 
         lax.fori_loop(lo, hi, body, 0)
 
     def comp_p(k, half, lo, hi):
         def body(j, carry):
-            here = lanes(j, 256)
-            wide = dot(HS[k, half], Ah[:, here])
-            value = wide[0:256] + wide[256:512] + dot(HS[k, half, pl.ds(0, 256), :], Al[:, here])
-            PX[k, pl.ds(8 * half, 8), :, :, here] = value.reshape(8, 4, 8, 256)
+            product(k, half, j)
             return carry
 
         lax.fori_loop(lo, hi, body, 0)
@@ -210,8 +213,12 @@
             self.sum_l = remote(relay.at[1], final.at[1, upper], *sem(2), left)
 
         def start(self):
-            for copy in (self.relay_r, self.relay_l, self.raw_r, self.raw_l):
-                copy.start()
+            self.relay_r.start()
+            self.relay_l.start()
+
+        def raw(self):
+            self.raw_r.start()
+            self.raw_l.start()
 
         def mid(self):
             for side, copy, chunk, onward in (
@@ -247,10 +254,10 @@
         def parts(base, h):
             return pl.ds(base + 4 * h, 4)
 
-        own_x1 = lambda t, h: PX.at[k, parts(0, h), t]
-        own_y1 = lambda t, h: PX.at[k, parts(8, h), :, :, lanes(t, 256)]
-        own_x2 = lambda t, h: PX.at[k, parts(0, h), x, :, lanes(t, 256)]
-        own_y2 = lambda t, h: PX.at[k, parts(8, h), t, :, lanes(y, 256)]
+        own_x1 = lambda t, h: PXX.at[k, t, parts(0, h)]
+        own_y1 = lambda t, h: PYY.at[k, t, parts(0, h)]
+        own_x2 = lambda t, h: PXX.at[k, x, parts(0, h), :, lanes(t, 256)]
+        own_y2 = lambda t, h: PYY.at[k, y, parts(0, h), t]
         first = (
             Ring(k, 0, own_x1, RLX.at[k], FNX.at[k], x, along_x, lambda h: own_x1(x, h)),
             Ring(k, 1, own_y1, RLY.at[k], FNY.at[k], y, along_y, lambda h: own_y1(y, h)),
@@ -267,6 +274,10 @@
         for i in which or (0, 1):
             ring[k][phase][i].start()
 
+    def rs_raw(k, phase, *which):
+        for i in which or (0, 1):
+            ring[k][phase][i].raw()
+
     def rs_mid(k, phase, *which):
         for i in which or (0, 1):
             ring[k][phase][i].mid()
@@ -275,23 +286,30 @@
         for i in which or (0, 1):
             ring[k][phase][i].end()
 
+    plane = sorted(
+        ((i, j) for i in range(4) for j in range(4) if i or j),
+        key=lambda p: -(min(p[0], 4 - p[0]) + min(p[1], 4 - p[1])),
+    )
+
     def begin(copy):
-        def body(o, carry):
+        for o in range(1, 16):
             copy(o).start()
-            return carry
-
-        lax.fori_loop(1, 16, body, 0)
+
+    def partner(o):
+        i, j = plane[o - 1]
+        return (x + i) % 4, (y + j) % 4
 
     def za(k):
         def copy(o):
-            to = (c + o) % 16
+            to = (c + 8 + (o // 2) * (2 * (o % 2) - 1)) % 16
             return remote(XS.at[to, k], ZB.at[c, k], sent.at[3], za_r.at[k], {"pcol": to})
 
         return copy
 
     def xa(k):
         def copy(o):
-            to = (r + o) % 16
+            px, py = partner(o)
+            to = px * 4 + py
             return remote(
                 ZB.at[to, k], XF.at[k, x, :, lanes(y, 256)], sent.at[4], xa_r.at[k], {"prow": to}
             )
@@ -327,9 +345,9 @@
         w = 128 * (3 - k)
 
         def copy(o):
-            to = (r + o) % 16
+            px, py = partner(o)
             return remote(
-                IN[k].at[to // 4, :, lanes(to % 4, w)], RB[k].at[o], sent.at[5], ra_r.at[k], {"prow": to}
+                IN[k].at[px, :, lanes(py, w)], RB[k].at[o], sent.at[5], ra_r.at[k], {"prow": px * 4 + py}
             )
 
         return copy
@@ -339,7 +357,8 @@
         mine = OU[k].at[x, :, lanes(y, w)]
 
         def copy(o):
-            return remote(mine, mine, sent.at[6], ga_r.at[k], {"prow": (r + o) % 16})
+            px, py = partner(o)
+            return remote(mine, mine, sent.at[6], ga_r.at[k], {"prow": px * 4 + py})
 
         return copy
 
@@ -366,10 +385,14 @@
 
     load_pan.wait()
     ag_start(0)
+    load_a.start()
+    load_c.start()
+    load_d.start()
+    load_f.start()
+    ag_step(0, 0)
     load_a.wait()
     prep_a(0)
     prep_a(1)
-    ag_step(0, 0)
     prep_a(2)
     prep_a(3)
     load_c.wait()
@@ -377,76 +400,106 @@
     ag_step(0, 1)
     ag_start(1)
     load_d.wait()
+    load_f.wait()
     prep_d()
     ag_step(0, 2)
     ag_step(1, 0)
     ag_step(0, 3)
+
+    @pl.when(core == 1)
+    def _():
+        ag_step(1, 1)
+
     ag_start(2)
     ag_end(0)
     comp_h(0)
-    ag_step(1, 1)
     comp_all(0, 0, 2)
+
+    @pl.when(core == 0)
+    def _():
+        ag_step(1, 1)
+
     ag_step(2, 0)
     comp_all(0, 2, 4)
     rs_start(0, 0)
     ag_step(1, 2)
-    comp_r(1, 0, 4)
+    comp_r(1, 0, 0, 2)
+    rs_raw(0, 0)
+    comp_r(1, 0, 2, 4)
     ag_step(2, 1)
+    comp_r(2, 0, 0, 2)
     ag_step(1, 3)
-    rs_mid(0, 0)
+
+    @pl.when(core == 1)
+    def _():
+        comp_r(2, 0, 2, 4)
+
     ag_end(1)
     comp_h(1)
     comp_all(1, 0, 2)
+    rs_mid(0, 0)
     ag_step(2, 2)
     comp_all(1, 2, 4)
+    rs_start(1, 0)
+
+    @pl.when(core == 0)
+    def _():
+        comp_r(2, 0, 2, 4)
+
+    rs_raw(1, 0)
+    comp_r(2, 1, 0, 4)
+    ag_step(2, 3)
     rs_end(0, 0)
     rs_start(0, 1)
-    rs_start(1, 0)
-    comp_r(2, 0, 2)
-    ag_step(2, 3)
-    rs_mid(0, 1)
-    comp_r(2, 2, 4)
+    rs_raw(0, 1)
     ag_end(2)
     comp_h(2)
     comp_p(2, 0, 0, 2)
     rs_mid(1, 0)
     comp_p(2, 0, 2, 4)
     rs_start(2, 0, 0)
-    comp_p(2, 1, 0, 4)
+    comp_p(2, 1, 0, 2)
+    rs_raw(2, 0, 0)
+    comp_p(2, 1, 2, 4)
     rs_start(2, 0, 1)
-    rs_end(0, 1)
-    za_start(0)
+    rs_raw(2, 0, 1)
+    rs_mid(0, 1)
     rs_end(1, 0)
     rs_start(1, 1)
+    rs_raw(1, 1)
     rs_mid(2, 0)
-    xa_start(0)
     rs_mid(1, 1)
     rs_end(2, 0, 0)
     rs_start(2, 1, 0)
+    rs_raw(2, 1, 0)
     rs_end(2, 0, 1)
     rs_start(2, 1, 1)
+    rs_raw(2, 1, 1)
+    rs_end(0, 1)
+    za_start(0)
     rs_end(1, 1)
     za_start(1)
     rs_mid(2, 1)
-    xa_end(0)
     rs_end(2, 1)
     za_start(2)
-    ar_start(0)
+    xa_start(0)
     xa_start(1)
     xa_start(2)
+    xa_end(0)
+    ar_start(0)
     xa_end(1)
     ar_start(1)
-    ar_mid(0)
     xa_end(2)
     ar_start(2)
+    ar_mid(0)
     ar_mid(1)
+    ar_mid(2)
     ar_end(0)
-    ar_mid(2)
     ar_end(1)
     ar_end(2)
 
     for i, ref in enumerate((
-        G.at[:, pl.ds(0, 7)], G.at[:, pl.ds(0, 8)], PX.at[:, pl.ds(0, 15)],
+        G.at[:, pl.ds(0, 7)], G.at[:, pl.ds(0, 8)], G.at[:, pl.ds(0, 15)],
         ZB.at[pl.ds(0, 15)], ZB.at[pl.ds(0, 15)], ZB.at[pl.ds(0, 15)], ZB.at[pl.ds(0, 15)],
     )):
         take(ref, sent.at[i])
@@ -469,11 +522,11 @@
     v = pltpu.VMEM
     sem = pltpu.SemaphoreType.DMA
     return [
-        v((3, 16, 32, 1024), F32), v((3, 2, 512, 1024), BF16),
+        v((3, 16, 32, 1024), F32), v((3, 2, 512, 1024), BF16), pltpu.SMEM((3, 128), jnp.int32),
         v((1024, 1024), F32), v((1024, 1024), BF16), v((1024, 1024), BF16),
         v((3, 512, 512), F32), v((3, 512, 512), F32), v((3, 512, 512), BF16), v((3, 512, 512), BF16),
-        v((512, 1024), F32),
-        v((3, 16, 4, 8, 1024), F32),
+        v((2, 512, 1024), F32),
+        v((3, 4, 8, 8, 1024), F32), v((3, 4, 8, 4, 8, 256), F32),
         v((3, 2, 4, 8, 1024), F32), v((3, 2, 8, 8, 1024), F32),
         v((3, 2, 4, 4, 8, 256), F32), v((3, 2, 8, 4, 8, 256), F32),
         v((3, 2, 4, 8, 256), F32), v((3, 2, 8, 8, 256), F32),
@@ -483,7 +536,7 @@
         v((16, 8, 384), F32), v((16, 8, 256), F32), v((16, 8, 128), F32),
         v((4, 8, 1536), F32), v((4, 8, 1024), F32), v((4, 8, 512), F32),
         v((6, 32, 512), F32),
-        sem((4,)), sem((2, 3, 4, 4)), sem((3,)), sem((3, 4, 3)),
+        sem((5,)), sem((2, 3, 4, 4)), sem((3,)), sem((3, 4, 3)),
         sem((3,)), sem((3,)), sem((3,)), sem((3,)), sem((7,)),
     ]
 
@@ -496,7 +549,7 @@
     held = pl.pallas_call(
         kernel,
         out_shape=results,
-        in_specs=[any_space, pl.BlockSpec(memory_space=pltpu.SMEM), any_space, any_space, any_space],
+        in_specs=[any_space] * 5,
         out_specs=(vmem, vmem, vmem),
         scratch_shapes=scratch(),
         compiler_params=pltpu.CompilerParams(

time: 102 us -> 100 us (0.980)
  Pallas kernels: 101 us -> 99.2 us
    pallas_call x1, Pallas kernels: 98.9 us -> 97.3 us  [shards(): pl.pallas_call(kernel, out_shape=results, in_specs=[any_space] * 5, out_s...]
where the time goes in v5:
time: 100 us
  Pallas kernels  99.2 us (99%)
    pallas_call x1, Pallas kernels, shards(): pl.pallas_call(kernel, out_shape=results, in_specs=[any_space] * 5, out_s...  97.3 us

profile of v5, /device:TPU:1, one launch (start us, length us, event | category | flops | bytes accessed | tf_op | source)
XLA Modules:
  0.0 100.0 jit_solution(9531223007766753120)
XLA Ops:
  0.6 97.3 %shard_map.76 = (f32[3,32,1024]{2,1,0:T(8,128)}, f32[3,32,512]{2,1,0:T(8,128)}, f32[3,32,512]{2,1,0:T(8,128)}) custom-call(f32[3,32,1024]{2,1,0:T(8,128)} %bitcast.2, s32[3,128]{1,0:T(4,128)} %pat.1, f32[3,512,512]{2,1,0:T(8,128)} %coup.1, f32[3,512,512]{2,1,0:T(8,128)} %dinv.1, f32[1024,1024]{1,0:T(8,128)} %ainv.1), custom_call_target="tpu_custom_call" | custom-call | tf_op jit(solution)/shard_map/pallas_call | solution.py:549
  97.9 1.9 %shard_map.77 = (f32[3,32,1024]{2,1,0:T(8,128)}, f32[3,32,512]{2,1,0:T(8,128)}, f32[3,32,512]{2,1,0:T(8,128)}) custom-call(f32[3,32,1024]{2,1,0:T(8,128)} %get-tuple-element.9.xt, f32[3,32,512]{2,1,0:T(8,128)} %get-tuple-element.10.xc, f32[3,32,512]{2,1,0:T(8,128)} %get-tuple-element.11.yd), custom_call_target="tpu_custom_call" | custom-call | tf_op jit(solution)/shard_map/pallas_call | solution.py:559

commit v6 on v5

--- a/solution.py
+++ b/solution.py
@@ -30,7 +30,7 @@
 def kernel(
     pan, pat, coup, dinv, ainv, xt_out, xc_out, yd_out,
     G, HS, flags, A32, Ah, Al, C32, D32, Ch, Cl, RM, PXX, PYY,
-    RLX, FNX, RLY, FNY, RLX2, FNX2, RLY2, FNY2,
+    RLX, FNX, RLY, FNY, RLX2, FNX2, RLY2, FNY2, FD,
     XS, ZB, XF, IN0, IN1, IN2, RB0, RB1, RB2, OU0, OU1, OU2, VD,
     load_sem, ag_r, pf_r, rs_r, za_r, xa_r, ra_r, ga_r, sent,
 ):
@@ -247,12 +247,34 @@
 
                 lax.fori_loop(0, 4, body, 0)
 
+    class Direct:
+        def __init__(self, k, phase, own, held, me, device, out):
+            self.own, self.held, self.me, self.out, self.done = own, held, me, out, rs_r.at[k, phase, 2]
+            self.copies = []
+            for i, step in enumerate((2, 1, 3)):
+                to = (me + step) % 4
+                self.copies.append(remote(own(to, None), held.at[i], sent.at[2], self.done, device(to)))
+
+        def start(self):
+            for copy in self.copies:
+                copy.start()
+
+        def end(self):
+            take(self.held, self.done)
+            mine, into = self.own(self.me, None), self.out(None)
+
+            def body(i, carry):
+                into[i] = mine[i] + self.held[0, i] + self.held[1, i] + self.held[2, i]
+                return carry
+
+            lax.fori_loop(0, 8, body, 0)
+
     along_x = lambda t: {"prow": t * 4 + y}
     along_y = lambda t: {"prow": x * 4 + t}
 
     def rings(k):
         def parts(base, h):
-            return pl.ds(base + 4 * h, 4)
+            return pl.ds(base, 8) if h is None else pl.ds(base + 4 * h, 4)
 
         own_x1 = lambda t, h: PXX.at[k, t, parts(0, h)]
         own_y1 = lambda t, h: PYY.at[k, t, parts(0, h)]
@@ -266,6 +288,11 @@
             Ring(k, 2, own_x2, RLX2.at[k], FNX2.at[k], y, along_y, lambda h: XS.at[parts(0, h), k]),
             Ring(k, 3, own_y2, RLY2.at[k], FNY2.at[k], x, along_x, lambda h: XS.at[parts(8, h), k]),
         )
+        if k == 2:
+            second = (
+                Direct(k, 2, own_x2, FD.at[0], y, along_y, lambda h: XS.at[parts(0, h), k]),
+                Direct(k, 3, own_y2, FD.at[1], x, along_x, lambda h: XS.at[parts(8, h), k]),
+            )
         return first, second
 
     ring = [rings(k) for k in range(3)]
@@ -469,17 +496,14 @@
     rs_raw(1, 1)
     rs_mid(2, 0)
     rs_mid(1, 1)
+    rs_end(0, 1)
+    za_start(0)
     rs_end(2, 0, 0)
     rs_start(2, 1, 0)
-    rs_raw(2, 1, 0)
     rs_end(2, 0, 1)
     rs_start(2, 1, 1)
-    rs_raw(2, 1, 1)
-    rs_end(0, 1)
-    za_start(0)
     rs_end(1, 1)
     za_start(1)
-    rs_mid(2, 1)
     rs_end(2, 1)
     za_start(2)
     xa_start(0)
@@ -531,6 +555,7 @@
         v((3, 2, 4, 4, 8, 256), F32), v((3, 2, 8, 4, 8, 256), F32),
         v((3, 2, 4, 8, 256), F32), v((3, 2, 8, 8, 256), F32),
         v((3, 2, 4, 8, 256), F32), v((3, 2, 8, 8, 256), F32),
+        v((2, 3, 8, 8, 256), F32),
         v((16, 3, 8, 256), F32), v((16, 3, 8, 256), F32), v((3, 4, 8, 1024), F32),
         v((4, 8, 1536), F32), v((4, 8, 1024), F32), v((4, 8, 512), F32),
         v((16, 8, 384), F32), v((16, 8, 256), F32), v((16, 8, 128), F32),

time: 100 us -> 97.9 us (0.979)
  Pallas kernels: 99.2 us -> 97 us
    pallas_call x1, Pallas kernels: 97.3 us -> 95.1 us  [shards(): pl.pallas_call(kernel, out_shape=results, in_specs=[any_space] * 5, out_s...]
where the time goes in v6:
time: 97.9 us; the launch traced here: 97.8 us
  Pallas kernels  97 us (99%)
    pallas_call x1, Pallas kernels, shards(): pl.pallas_call(kernel, out_shape=results, in_specs=[any_space] * 5, out_s...  95.1 us

profile of v6, /device:TPU:1, one launch (start us, length us, event | category | flops | bytes accessed | tf_op | source)
XLA Modules:
  0.0 97.8 jit_solution(14946157815325269747)
XLA Ops:
  0.6 95.1 %shard_map.76 = (f32[3,32,1024]{2,1,0:T(8,128)}, f32[3,32,512]{2,1,0:T(8,128)}, f32[3,32,512]{2,1,0:T(8,128)}) custom-call(f32[3,32,1024]{2,1,0:T(8,128)} %bitcast.2, s32[3,128]{1,0:T(4,128)} %pat.1, f32[3,512,512]{2,1,0:T(8,128)} %coup.1, f32[3,512,512]{2,1,0:T(8,128)} %dinv.1, f32[1024,1024]{1,0:T(8,128)} %ainv.1), custom_call_target="tpu_custom_call" | custom-call | tf_op jit(solution)/shard_map/pallas_call | solution.py:574
  95.7 1.9 %shard_map.77 = (f32[3,32,1024]{2,1,0:T(8,128)}, f32[3,32,512]{2,1,0:T(8,128)}, f32[3,32,512]{2,1,0:T(8,128)}) custom-call(f32[3,32,1024]{2,1,0:T(8,128)} %get-tuple-element.9.xt, f32[3,32,512]{2,1,0:T(8,128)} %get-tuple-element.10.xc, f32[3,32,512]{2,1,0:T(8,128)} %get-tuple-element.11.yd), custom_call_target="tpu_custom_call" | custom-call | tf_op jit(solution)/shard_map/pallas_call | solution.py:584
